TPU v7x, 256 devices: a whole 4x4x8 slice. The times are simulated.
256 devices in a mesh: grp: 8 (over y_lo, x), sx: 4 (over y_hi, core), sz: 8 (over z).
Axes of the slice: x: 4, y: 4 (y_hi: 2, y_lo: 2; y = y_hi * 2 + y_lo), z: 8, core: 2. Of those that a mesh axis runs over, the one named last changes fastest.
Arguments:
- radiant_density_before: float32 [16, 64, 128, 1024], P('grp', 'sx', None, 'sz'), may hold values from 0.2 to 6, as said below
- grain_kelvin_before: float32 [64, 128, 1024], P('sx', None, 'sz'), may hold values from 0.5 to 1.5
- grain_thermal_capacity: float32 [64, 128, 1024], P('sx', None, 'sz'), may hold values from 0.3 to 3
- grain_species_index: int32 [64, 128, 1024], P('sx', None, 'sz'), may hold values from 0 to 7
- band_absorptivity_table: float32 [8, 16], P(None, 'grp'), may hold values from 0.2 to 5
- blackbody_band_fraction: float32 [16], P('grp'), may hold values from 0.05 to 0.5
Outputs:
- radiant_density_after: float32 [16, 64, 128, 1024], P('grp', 'sx', None, 'sz')
- grain_kelvin_after: float32 [64, 128, 1024], P('sx', None, 'sz')
Inputs may be any that keep to these rules, and one draw needn't show every extreme that they name: `radiant_density_before`: positive everywhere.
All inputs are finite; a program needn't handle non-finite values.
Results may differ from a plain program's by a relative error of at most 0.0003.
Values sent between devices are 32-bit elements; how exact they have to be, the bound alone decides.
No kernel may reach another device: no remote copies, remote signals or barrier semaphores. Data moves between devices by JAX's collectives and lax.ppermute only.
A program may use at most 128 MiB of HBM per device.

v0:
```python
import functools

import jax
import jax.numpy as jnp
from jax import lax
from jax.experimental import pallas as pl
from jax.experimental.pallas import tpu as pltpu
from jax.sharding import PartitionSpec as P

DT = 0.5
SHIFT = 6.0
SCALE = 4.0
NX = 16
N = 128
MATS = 8
HE = 5
HT = 3
ROWS = 152
ZO = 12
RC = 8
NC = 136
PX = 24
CHUNKS = ((8, 48), (56, 48), (104, 40))
OWN = ((12, 48), (60, 48), (108, 32))

SX_A = [(0, 1), (1, 0), (2, 3), (3, 2)]
SX_B = [(1, 2), (2, 1), (3, 0), (0, 3)]
SZ_A = [(0, 1), (1, 0), (2, 3), (3, 2), (4, 5), (5, 4), (6, 7), (7, 6)]
SZ_B = [(1, 2), (2, 1), (3, 4), (4, 3), (5, 6), (6, 5), (7, 0), (0, 7)]

VM = pl.BlockSpec(memory_space=pltpu.VMEM)
SM = pl.BlockSpec(memory_space=pltpu.SMEM)
F32 = jnp.float32


def shaped(*dims):
    return jax.ShapeDtypeStruct(dims, F32)


def params(mib):
    return pltpu.CompilerParams(vmem_limit_bytes=mib * 1024 * 1024)


def cost(flops, nbytes):
    return pl.CostEstimate(flops=flops, bytes_accessed=nbytes, transcendentals=0)


def pick(species, values):
    b0, b1, b2 = ((species & k) != 0 for k in (1, 2, 4))
    level = [jnp.where(b0, values[2 * k + 1], values[2 * k]) for k in range(4)]
    level = [jnp.where(b1, level[1], level[0]), jnp.where(b1, level[3], level[2])]
    return jnp.where(b2, level[1], level[0])


def absorbed_kernel(e_ref, sp_ref, tab_ref, w_ref, out_ref):
    i = pl.program_id(0)
    tabs = [[tab_ref[m, g] for m in range(MATS)] for g in range(2)]

    @pl.when(i == 0)
    def _():
        for m in range(MATS):
            share = tabs[0][m] * w_ref[0] + tabs[1][m] * w_ref[1]
            for k in range(8):
                out_ref[k, NX, m : m + 1, :] = jnp.full((1, N), share, F32)
        for k in range(8):
            out_ref[k, NX, 8:16, :] = jnp.zeros((8, N), F32)

    for x in range(4):
        for k in range(4):
            rows = slice(k * 32, k * 32 + 32)
            species = sp_ref[x, rows, :]
            total = pick(species, tabs[0]) * e_ref[0, x, rows, :] + pick(species, tabs[1]) * e_ref[1, x, rows, :]
            out_ref[2 * k, i * 4 + x] = total[:16]
            out_ref[2 * k + 1, i * 4 + x] = total[16:]


def turn_kernel(e_ref, sp_ref, out_ref, a_ref, b_ref):
    i = pl.program_id(0)
    for x in range(2):
        for g in range(2):
            out_ref[g, i * 2 + x] = e_ref[g, x].T
        out_ref[2, i * 2 + x] = sp_ref[x].astype(F32).T

    @pl.when(i == pl.num_programs(0) - 1)
    def _():
        even = lax.rem(lax.axis_index("sx"), 2) == 0
        to_a = jnp.where(even, NX - HE, 0)
        to_b = jnp.where(even, 0, NX - HE)
        for c in range(3):
            for j in range(HE):
                a_ref[c, j] = out_ref[c, to_a + j]
                b_ref[c, j] = out_ref[c, to_b + j]


def edge_rows(get, depth, a_ref, b_ref):
    even = lax.rem(lax.axis_index("sz"), 2) == 0
    to_a = pl.multiple_of(jnp.where(even, N - 8, 0), 8)
    to_b = pl.multiple_of(jnp.where(even, 0, N - 8), 8)
    for x in range(depth):
        a_ref[x] = get(x, to_a)
        b_ref[x] = get(x, to_b)


def corner_kernel(c_count, halo, own_ref, xa_ref, xb_ref, a_ref, b_ref):
    even = lax.rem(lax.axis_index("sx"), 2) == 0
    for c in range(c_count):

        def fill(low, high):
            def get(x, row):
                if x < halo:
                    return low[c, x, pl.ds(row, 8), :]
                if x < halo + NX:
                    return own_ref[c, x - halo, pl.ds(row, 8), :]
                return high[c, x - halo - NX, pl.ds(row, 8), :]

            edge_rows(get, NX + 2 * halo, a_ref.at[c], b_ref.at[c])

        pl.when(even)(lambda: fill(xb_ref, xa_ref))
        pl.when(jnp.logical_not(even))(lambda: fill(xa_ref, xb_ref))


def assemble(c, halo, own_ref, xa_ref, xb_ref, za_ref, zb_ref, put):
    x_even = lax.rem(lax.axis_index("sx"), 2) == 0
    z_even = lax.rem(lax.axis_index("sz"), 2) == 0

    def copy(first, ref, offset, count, row):
        def step(j, carry):
            put(first + j, row, ref[c, offset + j])
            return carry

        lax.fori_loop(0, count, step, 0)

    copy(halo, own_ref, 0, NX, ZO)

    @pl.when(x_even)
    def _():
        copy(0, xb_ref, 0, halo, ZO)
        copy(halo + NX, xa_ref, 0, halo, ZO)

    @pl.when(jnp.logical_not(x_even))
    def _():
        copy(0, xa_ref, 0, halo, ZO)
        copy(halo + NX, xb_ref, 0, halo, ZO)

    @pl.when(z_even)
    def _():
        copy(0, zb_ref, 0, NX + 2 * halo, ZO - 8)
        copy(0, za_ref, 0, NX + 2 * halo, ZO + N)

    @pl.when(jnp.logical_not(z_even))
    def _():
        copy(0, za_ref, 0, NX + 2 * halo, ZO - 8)
        copy(0, zb_ref, 0, NX + 2 * halo, ZO + N)


def matrix_kernel(
    own_ref, xa_ref, xb_ref, za_ref, zb_ref, tab_ref, w_ref,
    dg_ref, kx_ref, ky_ref, kz_ref, q_ref, ow_ref,
    e_ref, sp_ref, d_ref, op_ref,
):
    sx, sz = lax.axis_index("sx"), lax.axis_index("sz")
    tabs = [[tab_ref[m, g] for m in range(MATS)] for g in range(2)]

    def put_e(g):
        def put(x, row, value):
            e_ref[g, x, row : row + value.shape[0], :] = value

        return put

    def put_s(x, row, value):
        sp_ref[x, row : row + value.shape[0], :] = value

    for c in range(3):
        assemble(c, HE, own_ref, xa_ref, xb_ref, za_ref, zb_ref, put_s if c == 2 else put_e(c))

    def clear_planes(first):
        def step(j, carry):
            for g in range(2):
                e_ref[g, first + j] = jnp.zeros((ROWS, N), F32)
            return carry

        lax.fori_loop(0, HE, step, 0)

    def clear_rows(row):
        def step(j, carry):
            for g in range(2):
                e_ref[g, j, row : row + 8, :] = jnp.zeros((8, N), F32)
            return carry

        lax.fori_loop(0, NX + 2 * HE, step, 0)

    pl.when(sx == 0)(lambda: clear_planes(0))
    pl.when(sx == 3)(lambda: clear_planes(HE + NX))
    pl.when(sz == 0)(lambda: clear_rows(ZO - 8))
    pl.when(sz == 7)(lambda: clear_rows(ZO + N))

    def lanes(n):
        return lax.broadcasted_iota(jnp.int32, (n, N), 1)

    def height(row, n):
        return lax.broadcasted_iota(jnp.int32, (n, N), 0) + (sz * N + row - ZO)

    def coefficients(p, carry):
        gx = sx * NX + p - 4
        x_in = jnp.logical_and(gx >= 0, gx < 4 * NX).astype(jnp.int32)
        for row, n in CHUNKS:
            gz = height(row, n)
            inside = jnp.logical_and(gz >= 0, gz < 8 * N * x_in)
            lane = lanes(n)
            rows = slice(row, row + n)
            species = sp_ref[p + 1, rows, :].astype(jnp.int32)
            for g in range(2):
                opacity = pick(species, tabs[g])
                center = e_ref[g, p + 1, rows, :]
                dx = e_ref[g, p + 2, rows, :] - e_ref[g, p, rows, :]
                dz = e_ref[g, p + 1, row + 1 : row + 1 + n, :] - e_ref[g, p + 1, row - 1 : row - 1 + n, :]
                above = jnp.where(lane == N - 1, 0.0, pltpu.roll(center, N - 1, 1))
                below = jnp.where(lane == 0, 0.0, pltpu.roll(center, 1, 1))
                dy = above - below
                square = 0.25 * (dx * dx + dy * dy + dz * dz)
                slope = jnp.sqrt(square)
                m = opacity * center
                upper = m * (2.0 * m + slope)
                lower = opacity * (m * (6.0 * m + 3.0 * slope) + square)
                d_ref[g, p, rows, :] = jnp.where(inside, upper / lower, 0.0)
                op_ref[g, p, rows, :] = opacity
        return carry

    lax.fori_loop(0, PX, coefficients, 0)

    inv = 1.0 / SCALE

    def operator(p, carry):
        gx = sx * NX + p - 4
        x_in = jnp.logical_and(gx >= 0, gx < 4 * NX).astype(jnp.int32)
        x_face = jnp.where(jnp.logical_and(gx >= 0, gx + 1 < 4 * NX), 0.5, 0.0)
        for row, n in CHUNKS:
            gz = height(row, n)
            inside = jnp.logical_and(gz >= 0, gz < 8 * N * x_in)
            z_face = jnp.where(jnp.logical_and(gz >= 0, gz + 1 < 8 * N), 0.5, 0.0)
            lane = lanes(n)
            rows = slice(row, row + n)
            up = slice(row + 1, row + 1 + n)
            down = slice(row - 1, row - 1 + n)
            for g in range(2):
                d = d_ref[g, p, rows, :]
                dxp, dxm = d_ref[g, p + 1, rows, :], d_ref[g, p - 1, rows, :]
                dzp, dzm = d_ref[g, p, up, :], d_ref[g, p, down, :]
                dyp = jnp.where(lane == N - 1, 0.0, pltpu.roll(d, N - 1, 1))
                dym = jnp.where(lane == 0, 0.0, pltpu.roll(d, 1, 1))
                opacity = op_ref[g, p, rows, :]
                sxp, sxm, szp, szm, syp, sym = (d + o for o in (dxp, dxm, dzp, dzm, dyp, dym))
                total = 0.5 * (((sxp + sxm) + (szp + szm)) + (syp + sym))
                diag = (1.0 / DT + opacity) + total
                center = e_ref[g, p + 1, rows, :]
                moved = (
                    (sxp * e_ref[g, p + 2, rows, :] + sxm * e_ref[g, p, rows, :])
                    + (szp * e_ref[g, p + 1, up, :] + szm * e_ref[g, p + 1, down, :])
                    + jnp.where(lane == N - 1, 0.0, syp * pltpu.roll(center, N - 1, 1))
                    + jnp.where(lane == 0, 0.0, sym * pltpu.roll(center, 1, 1))
                )
                q_ref[g, p, rows, :] = jnp.where(inside, (1.0 / DT - diag) * center + 0.5 * moved, 0.0)
                ow_ref[g, p, rows, :] = jnp.where(inside, opacity * w_ref[g], 0.0)
                dg_ref[g, p, rows, :] = jnp.where(inside, (diag - SHIFT) * inv, 0.0)
                kx_ref[g, p, rows, :] = sxp * (x_face * inv)
                kz_ref[g, p, rows, :] = szp * (z_face * inv)
                ky_ref[g, p, rows, :] = jnp.where(lane == N - 1, 0.0, syp * (0.5 * inv))
        return carry

    lax.fori_loop(1, PX - 1, operator, 0)


def temperature_kernel(g_ref, r_ref, t_ref, cap_ref, sp_ref, out_ref):
    shares = r_ref[0, NX, 0:8, :]
    for k in range(1, 8):
        shares = shares + r_ref[k, NX, 0:8, :]
    values = [jnp.broadcast_to(shares[m : m + 1, :], (16, N)) for m in range(MATS)]
    for x in range(NX):
        absorbed = r_ref[0, x]
        for k in range(1, 8):
            absorbed = absorbed + r_ref[k, x]
        t = t_ref[x]
        weight = pick(sp_ref[x], values)
        cube = t * t * t
        gain = absorbed - weight * (cube * t)
        slope = 4.0 * weight * cube
        after = t + DT * gain / (cap_ref[x] + DT * slope)
        for k in range(8):
            out_ref[k, x] = after


def emission_kernel(t_ref, out_ref, a_ref, b_ref):
    for x in range(NX):
        t = t_ref[:, x].reshape(N, N)
        square = t * t
        out_ref[0, x] = (square * square).T
    even = lax.rem(lax.axis_index("sx"), 2) == 0
    to_a = jnp.where(even, NX - HT, 0)
    to_b = jnp.where(even, 0, NX - HT)
    for j in range(HT):
        a_ref[0, j] = out_ref[0, to_a + j]
        b_ref[0, j] = out_ref[0, to_b + j]


def krylov_kernel(
    own_ref, xa_ref, xb_ref, za_ref, zb_ref, dg_ref, kx_ref, ky_ref, kz_ref, q_ref, ow_ref,
    v0_ref, v1_ref, v2_ref, mom_ref, t_ref,
):
    def put(x, row, value):
        t_ref[x, row : row + value.shape[0], :] = value

    assemble(0, HT, own_ref, xa_ref, xb_ref, za_ref, zb_ref, put)

    def first(p, carry):
        for row, n in CHUNKS:
            rows = slice(row, row + n)
            t = t_ref[p - 1, rows, :]
            for g in range(2):
                v0_ref[g, p, rows, :] = q_ref[g, p, rows, :] + ow_ref[g, p, rows, :] * t
        return carry

    lax.fori_loop(1, PX - 1, first, 0)

    def apply(v_ref, g, p, row, n):
        rows = slice(row, row + n)
        up = slice(row + 1, row + 1 + n)
        down = slice(row - 1, row - 1 + n)
        c = v_ref[g, p, rows, :]
        ky = ky_ref[g, p, rows, :]
        total = dg_ref[g, p, rows, :] * c
        total = total - kx_ref[g, p, rows, :] * v_ref[g, p + 1, rows, :]
        total = total - kx_ref[g, p - 1, rows, :] * v_ref[g, p - 1, rows, :]
        total = total - kz_ref[g, p, rows, :] * v_ref[g, p, up, :]
        total = total - kz_ref[g, p, down, :] * v_ref[g, p, down, :]
        total = total - ky * pltpu.roll(c, N - 1, 1)
        return total - pltpu.roll(ky * c, 1, 1)

    for source, target, start in ((v0_ref, v1_ref, 2), (v1_ref, v2_ref, 3)):

        def step(p, carry, source=source, target=target):
            for g in range(2):
                for row, n in CHUNKS:
                    target[g, p, row : row + n, :] = apply(source, g, p, row, n)
            return carry

        lax.fori_loop(start, PX - start, step, 0)

    def fold(value):
        return jnp.sum(value.reshape(-1, 8, N), axis=0)

    for g in range(2):

        def last(p, sums, g=g):
            sums = list(sums)
            for row, n in OWN:
                rows = slice(row, row + n)
                a, b, c = v0_ref[g, p, rows, :], v1_ref[g, p, rows, :], v2_ref[g, p, rows, :]
                d = apply(v2_ref, g, p, row, n)
                for k, (l, r) in enumerate(((a, a), (a, b), (b, b), (b, c), (c, c), (c, d))):
                    sums[k] = sums[k] + fold(l * r)
            return tuple(sums)

        sums = lax.fori_loop(4, 4 + NX, last, (jnp.zeros((8, N), F32),) * 6)
        for k in range(6):
            line = jnp.sum(sums[k], axis=0, keepdims=True)
            for peer in range(mom_ref.shape[0]):
                mom_ref[peer, g * 8 + k : g * 8 + k + 1, :] = line
        for peer in range(mom_ref.shape[0]):
            mom_ref[peer, g * 8 + 6 : g * 8 + 8, :] = jnp.zeros((2, N), F32)


def turn_back_kernel(v0_ref, v1_ref, v2_ref, out_ref):
    for k, ref in enumerate((v0_ref, v1_ref, v2_ref)):

        def step(x, carry, k=k, ref=ref):
            for g in range(2):
                out_ref[k, g, x] = ref[g, x + 4, ZO : ZO + N, :].T
            return carry

        lax.fori_loop(0, NX, step, 0)


def update_kernel(mom_ref, e_ref, v_ref, out_ref, c_ref):
    @pl.when(pl.program_id(0) == 0)
    def _():
        total = mom_ref[0]
        for k in range(1, mom_ref.shape[0]):
            total = total + mom_ref[k]
        total = jnp.sum(total, axis=1, keepdims=True)
        for g in range(2):
            n = [total[g * 8 + k : g * 8 + k + 1, :] for k in range(6)]
            m = [SHIFT * n[k] + SCALE * n[k + 1] for k in range(5)]
            l1 = m[1] / m[0]
            l2 = m[2] / m[0]
            p1 = m[2] - l1 * m[1]
            u = m[3] - l1 * m[2]
            r1 = n[1] - l1 * n[0]
            ok1 = p1 > 1e-6 * m[2]
            s1 = jnp.where(ok1, u / p1, 0.0)
            p2 = m[4] - l2 * m[2] - s1 * u
            r2 = n[2] - l2 * n[0] - s1 * r1
            ok2 = jnp.logical_and(ok1, p2 > 1e-6 * m[4])
            c2 = jnp.where(ok2, r2 / p2, 0.0)
            c1 = jnp.where(ok1, (r1 - u * c2) / p1, 0.0)
            c0 = (n[0] - m[1] * c1 - m[2] * c2) / m[0]
            for k, c in enumerate((c0, c1, c2)):
                c_ref[g * 3 + k] = jnp.broadcast_to(c, (8, N))

    for x in range(4):
        for g in range(2):
            total = e_ref[g, x]
            for k in range(3):
                total = total + v_ref[k, g, x] * c_ref[g * 3 + k, 0:1, :]
            out_ref[g, x] = total


def exchange(a, b, axis, pair_a, pair_b):
    return lax.ppermute(a, axis, pair_a), lax.ppermute(b, axis, pair_b)


def shards(energy, kelvin, capacity, species, table, fraction):
    planes = lambda k: pl.BlockSpec((2, k, N, N), lambda i: (0, i, 0, 0))
    single = lambda k: pl.BlockSpec((k, N, N), lambda i: (i, 0, 0))
    whole = lambda *d: pl.BlockSpec(d, lambda *_: (0,) * len(d))

    absorbed = pl.pallas_call(
        absorbed_kernel,
        out_shape=shaped(8, NX + 1, 16, N),
        grid=(4,),
        in_specs=[planes(4), single(4), SM, SM],
        out_specs=whole(8, NX + 1, 16, N),
        compiler_params=params(8),
        cost_estimate=cost(10_000_000, 4_000_000),
        name="absorbed",
    )(energy, species, table, fraction)
    gathered = lax.all_to_all(absorbed, "grp", 0, 0, tiled=True)

    own, xa, xb = pl.pallas_call(
        turn_kernel,
        out_shape=(shaped(3, NX, N, N), shaped(3, HE, N, N), shaped(3, HE, N, N)),
        grid=(8,),
        in_specs=[planes(2), single(2)],
        out_specs=(whole(3, NX, N, N), whole(3, HE, N, N), whole(3, HE, N, N)),
        compiler_params=params(14),
        cost_estimate=cost(10_000_000, 8_000_000),
        name="turn",
    )(energy, species)
    xa, xb = exchange(xa, xb, "sx", SX_A, SX_B)
    za, zb = pl.pallas_call(
        functools.partial(corner_kernel, 3, HE),
        out_shape=(shaped(3, NX + 2 * HE, 8, N),) * 2,
        in_specs=[VM] * 3,
        out_specs=(VM, VM),
        compiler_params=params(8),
        cost_estimate=cost(1000, 1_000_000),
        name="corners",
    )(own, xa, xb)
    za, zb = exchange(za, zb, "sz", SZ_A, SZ_B)
    field = shaped(2, PX, ROWS, N)
    scratch = pltpu.VMEM((2, PX, ROWS, N), F32)
    coefs = pl.pallas_call(
        matrix_kernel,
        out_shape=(field,) * 6,
        in_specs=[VM] * 5 + [SM, SM],
        out_specs=(VM,) * 6,
        scratch_shapes=[
            pltpu.VMEM((2, NX + 2 * HE, ROWS, N), F32),
            pltpu.VMEM((NX + 2 * HE, ROWS, N), F32),
            scratch,
            scratch,
        ],
        compiler_params=params(50),
        cost_estimate=cost(100_000_000, 30_000_000),
        name="matrix",
    )(own, xa, xb, za, zb, table, fraction)

    share = pl.BlockSpec((NX, 16, N), lambda i, g: (0, g[0], 0))
    where = lax.axis_index("grp").astype(jnp.int32).reshape(1)
    after = pl.pallas_call(
        temperature_kernel,
        out_shape=shaped(8, NX, 16, N),
        grid_spec=pltpu.PrefetchScalarGridSpec(
            num_scalar_prefetch=1,
            grid=(1,),
            in_specs=[whole(8, NX + 1, 16, N), share, share, share],
            out_specs=whole(8, NX, 16, N),
        ),
        compiler_params=params(8),
        cost_estimate=cost(1_000_000, 3_000_000),
        name="temperature",
    )(where, gathered, kelvin, capacity, species)
    after = lax.all_to_all(after, "grp", 0, 0, tiled=True)
    kelvin_after = jnp.moveaxis(after, 0, 1).reshape(NX, N, N)

    own_t, ta, tb = pl.pallas_call(
        emission_kernel,
        out_shape=(shaped(1, NX, N, N), shaped(1, HT, N, N), shaped(1, HT, N, N)),
        in_specs=[VM],
        out_specs=(VM,) * 3,
        compiler_params=params(8),
        cost_estimate=cost(1_000_000, 3_000_000),
        name="emission",
    )(after)
    ta, tb = exchange(ta, tb, "sx", SX_A, SX_B)
    tza, tzb = pl.pallas_call(
        functools.partial(corner_kernel, 1, HT),
        out_shape=(shaped(1, NX + 2 * HT, 8, N),) * 2,
        in_specs=[VM] * 3,
        out_specs=(VM, VM),
        compiler_params=params(8),
        cost_estimate=cost(1000, 300_000),
        name="corners_t",
    )(own_t, ta, tb)
    tza, tzb = exchange(tza, tzb, "sz", SZ_A, SZ_B)

    v0, v1, v2, mom = pl.pallas_call(
        krylov_kernel,
        out_shape=(field, field, field, shaped(32, 16, N)),
        in_specs=[VM] * 11,
        out_specs=(VM,) * 4,
        scratch_shapes=[pltpu.VMEM((NX + 2 * HT, ROWS, N), F32)],
        compiler_params=params(50),
        cost_estimate=cost(100_000_000, 30_000_000),
        name="krylov",
    )(own_t, ta, tb, tza, tzb, *coefs)
    mom = lax.all_to_all(mom, ("sx", "sz"), 0, 0, tiled=True)
    turned = pl.pallas_call(
        turn_back_kernel,
        out_shape=shaped(3, 2, NX, N, N),
        in_specs=[VM] * 3,
        out_specs=VM,
        compiler_params=params(30),
        cost_estimate=cost(10_000_000, 12_000_000),
        name="turn_back",
    )(v0, v1, v2)
    result = pl.pallas_call(
        update_kernel,
        out_shape=shaped(2, NX, N, N),
        grid=(4,),
        in_specs=[
            whole(32, 16, N),
            planes(4),
            pl.BlockSpec((3, 2, 4, N, N), lambda i: (0, 0, i, 0, 0)),
        ],
        out_specs=planes(4),
        scratch_shapes=[pltpu.VMEM((6, 8, N), F32)],
        compiler_params=params(16),
        cost_estimate=cost(10_000_000, 10_000_000),
        name="update",
    )(mom, energy, turned)
    return result, kelvin_after


def solution(mesh):
    placed = (
        P("grp", "sx", None, "sz"),
        P("sx", None, "sz"),
        P("sx", None, "sz"),
        P("sx", None, "sz"),
        P(None, "grp"),
        P("grp"),
    )
    return jax.shard_map(
        shards,
        mesh=mesh,
        in_specs=placed,
        out_specs=(P("grp", "sx", None, "sz"), P("sx", None, "sz")),
        check_vma=False,
    )
```

profile of v0, /device:TPU:1, one launch (start us, length us, event | category | flops | bytes accessed | tf_op | source)
XLA Modules:
  0.0 152.5 jit_solution(9295419049342695974)
XLA Ops:
  0.6 0.8 copy.10.tab_ref
  1.4 1.6 %copy-done.2 = f32[2,16,128,128]{3,2,1,0:T(8,128)S(1)} copy-done((f32[2,16,128,128]{3,2,1,0:T(8,128)S(1)}, f32[2,16,128,128]{3,2,1,0:T(8,128)}, u32[]{:S(2)}) %copy-start.2) | copy-done | bytes 2097176
  3.0 1.2 copy-done.6
  4.2 0.7 copy-done.16
  4.9 1.7 %absorbed.1 = f32[8,17,16,128]{3,2,1,0:T(8,128)S(1)} custom-call(f32[2,16,128,128]{3,2,1,0:T(8,128)S(1)} %copy-done.2, s32[16,128,128]{2,1,0:T(8,128)S(1)} %copy-done.6, f32[8,2]{1,0:T(8,128)S(1)} %copy.10.tab_ref, f32[2]{0:T(128)S(1)} %copy-done.16), custom_call_target="tpu_custom_call" | custom-call | flops 10000000 | bytes 4000000 | tf_op jit(solution)/shard_map/absorbed/pallas_call | solution.py:426
  6.6 0.0 copy-start.8
  6.6 1.0 copy-done.8
  7.6 5.9 %all-to-all-start = ((f32[8,17,16,128]{3,2,1,0:T(8,128)}), f32[8,17,16,128]{3,2,1,0:T(8,128)}, u32[]{:S(2)}, u32[]{:S(2)}) async-start(f32[8,17,16,128]{3,2,1,0:T(8,128)} %copy-done.8), calls=%async_computation | async-start | bytes 2228224 | tf_op jit(solution)/shard_map/all_to_all | solution.py:436
  13.4 3.0 %turn.1 = (f32[3,16,128,128]{3,2,1,0:T(8,128)S(1)}, f32[3,5,128,128]{3,2,1,0:T(8,128)}, f32[3,5,128,128]{3,2,1,0:T(8,128)}) custom-call(f32[2,16,128,128]{3,2,1,0:T(8,128)S(1)} %copy-done.3, s32[16,128,128]{2,1,0:T(8,128)S(1)} %copy-done.7), custom_call_target="tpu_custom_call" | custom-call | flops 10000000 | bytes 8000000 | tf_op jit(solution)/shard_map/turn/pallas_call | solution.py:438
  16.4 1.7 %copy-done.4 = f32[3,16,128,128]{3,2,1,0:T(8,128)} copy-done((f32[3,16,128,128]{3,2,1,0:T(8,128)}, f32[3,16,128,128]{3,2,1,0:T(8,128)S(1)}, u32[]{:S(2)}) %copy-start.4) | copy-done | bytes 3145752
  18.1 1.6 %collective-permute-start.4 = (f32[3,5,128,128]{3,2,1,0:T(8,128)}, f32[3,5,128,128]{3,2,1,0:T(8,128)}, u32[]{:S(2)}, u32[]{:S(2)}) collective-permute-start(f32[3,5,128,128]{3,2,1,0:T(8,128)} %get-tuple-element.28), channel_id=1, source_target_pairs={{0,8},{8,0},{16,24},{24,16},{1,9},{9,1},{17,25},{25,17},{2,10},{10... | collective-permute-start | bytes 2949128 | tf_op jit(solution)/shard_map/ppermute | solution.py:418
  19.7 1.9 %collective-permute-start.5 = (f32[3,5,128,128]{3,2,1,0:T(8,128)}, f32[3,5,128,128]{3,2,1,0:T(8,128)}, u32[]{:S(2)}, u32[]{:S(2)}) collective-permute-start(f32[3,5,128,128]{3,2,1,0:T(8,128)} %get-tuple-element.29), channel_id=1, source_target_pairs={{8,16},{16,8},{24,0},{0,24},{9,17},{17,9},{25,1},{1,25},{10,18},{1... | collective-permute-start | bytes 2949128 | tf_op jit(solution)/shard_map/ppermute | solution.py:418
  21.6 8.5 %all-to-all-done.r_ref = f32[8,17,16,128]{3,2,1,0:T(8,128)} async-done(((f32[8,17,16,128]{3,2,1,0:T(8,128)}), f32[8,17,16,128]{3,2,1,0:T(8,128)}, u32[]{:S(2)}, u32[]{:S(2)}) %all-to-all-start) | async-done | bytes 1114144 | tf_op jit(solution)/shard_map/all_to_all | solution.py:436
  30.1 1.2 copy-done.13
  31.3 1.2 copy-done.14
  32.6 1.4 temperature.1
  34.0 0.0 copy-start.9
  34.0 1.0 copy-done.9
  34.9 3.6 %all-to-all-start.1 = ((f32[8,16,16,128]{3,2,1,0:T(8,128)}), f32[8,16,16,128]{3,2,1,0:T(8,128)S(1)}, u32[]{:S(2)}, u32[]{:S(2)}) async-start(f32[8,16,16,128]{3,2,1,0:T(8,128)} %copy-done.9), calls=%async_computation.1 | async-start | bytes 2097152 | tf_op jit(solution)/shard_map/all_to_all | solution.py:492
  38.5 0.0 collective-permute-done.4.xa_ref
  38.5 21.1 %collective-permute-done.5.xb_ref = f32[3,5,128,128]{3,2,1,0:T(8,128)} collective-permute-done((f32[3,5,128,128]{3,2,1,0:T(8,128)}, f32[3,5,128,128]{3,2,1,0:T(8,128)}, u32[]{:S(2)}, u32[]{:S(2)}) %collective-permute-start.5) | collective-permute-done | bytes 983072 | tf_op jit(solution)/shard_map/ppermute | solution.py:418
  59.6 1.9 %copy-done.5 = f32[3,16,128,128]{3,2,1,0:T(8,128)S(1)} copy-done((f32[3,16,128,128]{3,2,1,0:T(8,128)S(1)}, f32[3,16,128,128]{3,2,1,0:T(8,128)}, u32[]{:S(2)}) %copy-start.5) | copy-done | bytes 3145752
  61.5 2.4 %corners.1 = (f32[3,26,8,128]{3,2,1,0:T(8,128)}, f32[3,26,8,128]{3,2,1,0:T(8,128)}) custom-call(f32[3,16,128,128]{3,2,1,0:T(8,128)S(1)} %copy-done.5, f32[3,5,128,128]{3,2,1,0:T(8,128)} %collective-permute-done.4.xa_ref, f32[3,5,128,128]{3,2,1,0:T(8,128)} %collective-permute-done.5.xb_ref), custom_call_target="tpu_custom_call" | custom-call | flops 1000 | bytes 1000000 | tf_op jit(solution)/shard_map/corners/pallas_call | solution.py:449
  63.9 1.6 %collective-permute-start.6 = (f32[3,26,8,128]{3,2,1,0:T(8,128)}, f32[3,26,8,128]{3,2,1,0:T(8,128)S(1)}, u32[]{:S(2)}, u32[]{:S(2)}) collective-permute-start(f32[3,26,8,128]{3,2,1,0:T(8,128)} %get-tuple-element.30), channel_id=1, source_target_pairs={{0,1},{1,0},{2,3},{3,2},{4,5},{5,4},{6,7},{7,6},{8,9},{9,8},{10,11... | collective-permute-start | bytes 958472 | tf_op jit(solution)/shard_map/ppermute | solution.py:418
  65.5 4.7 %collective-permute-start.7 = (f32[3,26,8,128]{3,2,1,0:T(8,128)}, f32[3,26,8,128]{3,2,1,0:T(8,128)}, u32[]{:S(2)}, u32[]{:S(2)}) collective-permute-start(f32[3,26,8,128]{3,2,1,0:T(8,128)} %get-tuple-element.31), channel_id=1, source_target_pairs={{1,2},{2,1},{3,4},{4,3},{5,6},{6,5},{7,0},{0,7},{9,10},{10,9},{11,... | collective-permute-start | bytes 958472 | tf_op jit(solution)/shard_map/ppermute | solution.py:418
  70.2 0.0 all-to-all-done.1.t_ref
  70.2 0.4 emission.1
  70.6 1.1 collective-permute-start
  71.6 0.3 collective-permute-start.1
  72.0 0.7 collective-permute-done.xa_ref
  72.7 7.0 %collective-permute-done.1.xb_ref = f32[1,3,128,128]{3,2,1,0:T(8,128)S(1)} collective-permute-done((f32[1,3,128,128]{3,2,1,0:T(8,128)S(1)}, f32[1,3,128,128]{3,2,1,0:T(8,128)S(1)}, u32[]{:S(2)}, u32[]{:S(2)}) %collective-permute-start.1) | collective-permute-done | bytes 196640 | tf_op jit(solution)/shard_map/ppermute | solution.py:418
  79.8 0.1 collective-permute-start.2
  79.9 1.4 collective-permute-start.3
  81.3 0.0 collective-permute-done.6.za_ref
  81.3 0.0 collective-permute-done.7.zb_ref
  81.3 23.4 %matrix.1 = (f32[2,24,152,128]{3,2,1,0:T(8,128)}, f32[2,24,152,128]{3,2,1,0:T(8,128)}, f32[2,24,152,128]{3,2,1,0:T(8,128)}, f32[2,24,152,128]{3,2,1,0:T(8,128)},...) custom-call(f32[3,16,128,128]{3,2,1,0:T(8,128)} %copy-done.4, ...), custom_call_target="tpu_custom_call" | custom-call | flops 100000000 | bytes 30000000 | tf_op jit(solution)/shard_map/matrix/pallas_call | solution.py:461
  104.8 0.0 collective-permute-done.2.za_ref
  104.8 22.2 %krylov.1 = (f32[2,24,152,128]{3,2,1,0:T(8,128)}, f32[2,24,152,128]{3,2,1,0:T(8,128)}, f32[2,24,152,128]{3,2,1,0:T(8,128)}, f32[32,16,128]{2,1,0:T(8,128)S(1)}) custom-call(f32[1,16,128,128]{3,2,1,0:T(8,128)S(1)} %get-tuple-element.22.own_ref, f32[1,3,128,128]{3,2,1,0:T(8,128)S(1)} %collective-permute-done.xa_ref, ...), custom_call_target="tpu_custom_call" | custom-call | flops 100000000 | bytes 30000000 | tf_op jit(solution)/shard_map/krylov/pallas_call | solution.py:516
  127.0 0.7 copy-done.15
  127.7 4.7 %all-to-all-start.2 = ((f32[32,16,128]{2,1,0:T(8,128)}), f32[32,16,128]{2,1,0:T(8,128)S(1)}, u32[]{:S(2)}, u32[]{:S(2)}) async-start(f32[32,16,128]{2,1,0:T(8,128)} %copy-done.15), calls=%async_computation.2 | async-start | bytes 524288 | tf_op jit(solution)/shard_map/all_to_all | solution.py:526
  132.4 1.1 copy.12
  133.5 2.1 %copy-done.10 = f32[2,24,152,128]{3,2,1,0:T(8,128)S(1)} copy-done((f32[2,24,152,128]{3,2,1,0:T(8,128)S(1)}, f32[2,24,152,128]{3,2,1,0:T(8,128)}, u32[]{:S(2)}) %copy-start.10) | copy-done | bytes 3735576
  135.6 2.1 %copy-done.11 = f32[2,24,152,128]{3,2,1,0:T(8,128)S(1)} copy-done((f32[2,24,152,128]{3,2,1,0:T(8,128)S(1)}, f32[2,24,152,128]{3,2,1,0:T(8,128)}, u32[]{:S(2)}) %copy-start.11) | copy-done | bytes 3735576
  137.6 2.1 %copy-done.12 = f32[2,24,152,128]{3,2,1,0:T(8,128)S(1)} copy-done((f32[2,24,152,128]{3,2,1,0:T(8,128)S(1)}, f32[2,24,152,128]{3,2,1,0:T(8,128)}, u32[]{:S(2)}) %copy-start.12) | copy-done | bytes 3735576
  139.7 4.8 %turn_back.1.v_ref = f32[3,2,16,128,128]{4,3,2,1,0:T(8,128)S(1)} custom-call(f32[2,24,152,128]{3,2,1,0:T(8,128)S(1)} %copy-done.10, f32[2,24,152,128]{3,2,1,0:T(8,128)S(1)} %copy-done.11, f32[2,24,152,128]{3,2,1,0:T(8,128)S(1)} %copy-done.12), custom_call_target="tpu_custom_call" | custom-call | flops 10000000 | bytes 12000000 | tf_op jit(solution)/shard_map/turn_back/pallas_call | solution.py:527
  144.5 2.6 %copy-done = f32[3,2,16,128,128]{4,3,2,1,0:T(8,128)} copy-done((f32[3,2,16,128,128]{4,3,2,1,0:T(8,128)}, f32[3,2,16,128,128]{4,3,2,1,0:T(8,128)S(1)}, u32[]{:S(2)}) %copy-start) | copy-done | bytes 6291480
  147.1 2.8 %copy-done.1 = f32[3,2,16,128,128]{4,3,2,1,0:T(8,128)S(1)} copy-done((f32[3,2,16,128,128]{4,3,2,1,0:T(8,128)S(1)}, f32[3,2,16,128,128]{4,3,2,1,0:T(8,128)}, u32[]{:S(2)}) %copy-start.1) | copy-done | bytes 6291480
  149.9 2.6 %update.1 = f32[2,16,128,128]{3,2,1,0:T(8,128)} custom-call(f32[32,16,128]{2,1,0:T(8,128)S(1)} %all-to-all-done.2.mom_ref, f32[2,16,128,128]{3,2,1,0:T(8,128)S(1)} %copy-done.3, f32[3,2,16,128,128]{4,3,2,1,0:T(8,128)S(1)} %copy-done.1), custom_call_target="tpu_custom_call" | custom-call | flops 10000000 | bytes 10000000 | tf_op jit(solution)/shard_map/update/pallas_call | solution.py:536
  (22 shorter events, 0.1 us)
Async XLA Ops:
  1.4 1.6 %copy-start.2 = (f32[2,16,128,128]{3,2,1,0:T(8,128)S(1)}, f32[2,16,128,128]{3,2,1,0:T(8,128)}, u32[]{:S(2)}) copy-start(f32[2,16,128,128]{3,2,1,0:T(8,128)} %e_ref.5) | copy-start | bytes 6291460
  3.0 1.2 copy-start.6
  4.2 0.7 copy-start.16
  4.9 8.6 %copy-start.3 = (f32[2,16,128,128]{3,2,1,0:T(8,128)S(1)}, f32[2,16,128,128]{3,2,1,0:T(8,128)}, u32[]{:S(2)}) copy-start(f32[2,16,128,128]{3,2,1,0:T(8,128)} %e_ref.5) | copy-start | bytes 6291460
  4.9 8.6 %copy-start.7 = (s32[16,128,128]{2,1,0:T(8,128)S(1)}, s32[16,128,128]{2,1,0:T(8,128)}, u32[]{:S(2)}) copy-start(s32[16,128,128]{2,1,0:T(8,128)} %sp_ref.5) | copy-start | bytes 3145732
  6.6 1.0 copy-start.8
  7.6 22.5 %all-to-all-start = ((f32[8,17,16,128]{3,2,1,0:T(8,128)}), f32[8,17,16,128]{3,2,1,0:T(8,128)}, u32[]{:S(2)}, u32[]{:S(2)}) async-start(f32[8,17,16,128]{3,2,1,0:T(8,128)} %copy-done.8), calls=%async_computation | async-start | bytes 2228224 | tf_op jit(solution)/shard_map/all_to_all | solution.py:436
  16.4 1.7 %copy-start.4 = (f32[3,16,128,128]{3,2,1,0:T(8,128)}, f32[3,16,128,128]{3,2,1,0:T(8,128)S(1)}, u32[]{:S(2)}) copy-start(f32[3,16,128,128]{3,2,1,0:T(8,128)S(1)} %get-tuple-element.27.own_ref) | copy-start | bytes 9437188
  18.1 20.4 %collective-permute-start.4 = (f32[3,5,128,128]{3,2,1,0:T(8,128)}, f32[3,5,128,128]{3,2,1,0:T(8,128)}, u32[]{:S(2)}, u32[]{:S(2)}) collective-permute-start(f32[3,5,128,128]{3,2,1,0:T(8,128)} %get-tuple-element.28), channel_id=1, source_target_pairs={{0,8},{8,0},{16,24},{24,16},{1,9},{9,1},{17,25},{25,17},{2,10},{10... | collective-permute-start | bytes 2949128 | tf_op jit(solution)/shard_map/ppermute | solution.py:418
  19.7 39.8 %collective-permute-start.5 = (f32[3,5,128,128]{3,2,1,0:T(8,128)}, f32[3,5,128,128]{3,2,1,0:T(8,128)}, u32[]{:S(2)}, u32[]{:S(2)}) collective-permute-start(f32[3,5,128,128]{3,2,1,0:T(8,128)} %get-tuple-element.29), channel_id=1, source_target_pairs={{8,16},{16,8},{24,0},{0,24},{9,17},{17,9},{25,1},{1,25},{10,18},{1... | collective-permute-start | bytes 2949128 | tf_op jit(solution)/shard_map/ppermute | solution.py:418
  30.1 1.2 copy-start.13
  31.3 1.2 copy-start.14
  34.0 1.0 copy-start.9
  34.9 35.3 %all-to-all-start.1 = ((f32[8,16,16,128]{3,2,1,0:T(8,128)}), f32[8,16,16,128]{3,2,1,0:T(8,128)S(1)}, u32[]{:S(2)}, u32[]{:S(2)}) async-start(f32[8,16,16,128]{3,2,1,0:T(8,128)} %copy-done.9), calls=%async_computation.1 | async-start | bytes 2097152 | tf_op jit(solution)/shard_map/all_to_all | solution.py:492
  59.6 1.9 %copy-start.5 = (f32[3,16,128,128]{3,2,1,0:T(8,128)S(1)}, f32[3,16,128,128]{3,2,1,0:T(8,128)}, u32[]{:S(2)}) copy-start(f32[3,16,128,128]{3,2,1,0:T(8,128)} %copy-done.4) | copy-start | bytes 9437188
  61.5 19.9 %copy-start.17 = (f32[2]{0:T(128)S(1)}, f32[2]{0:T(128)}, u32[]{:S(2)}) copy-start(f32[2]{0:T(128)} %w_ref.3) | copy-start | bytes 28
  63.9 17.4 %collective-permute-start.6 = (f32[3,26,8,128]{3,2,1,0:T(8,128)}, f32[3,26,8,128]{3,2,1,0:T(8,128)S(1)}, u32[]{:S(2)}, u32[]{:S(2)}) collective-permute-start(f32[3,26,8,128]{3,2,1,0:T(8,128)} %get-tuple-element.30), channel_id=1, source_target_pairs={{0,1},{1,0},{2,3},{3,2},{4,5},{5,4},{6,7},{7,6},{8,9},{9,8},{10,11... | collective-permute-start | bytes 958472 | tf_op jit(solution)/shard_map/ppermute | solution.py:418
  65.5 15.8 %collective-permute-start.7 = (f32[3,26,8,128]{3,2,1,0:T(8,128)}, f32[3,26,8,128]{3,2,1,0:T(8,128)}, u32[]{:S(2)}, u32[]{:S(2)}) collective-permute-start(f32[3,26,8,128]{3,2,1,0:T(8,128)} %get-tuple-element.31), channel_id=1, source_target_pairs={{1,2},{2,1},{3,4},{4,3},{5,6},{6,5},{7,0},{0,7},{9,10},{10,9},{11,... | collective-permute-start | bytes 958472 | tf_op jit(solution)/shard_map/ppermute | solution.py:418
  70.6 2.1 %collective-permute-start = (f32[1,3,128,128]{3,2,1,0:T(8,128)S(1)}, f32[1,3,128,128]{3,2,1,0:T(8,128)S(1)}, u32[]{:S(2)}, u32[]{:S(2)}) collective-permute-start(f32[1,3,128,128]{3,2,1,0:T(8,128)S(1)} %get-tuple-element.23), channel_id=1, source_target_pairs={{0,8},{8,0},{16,24},{24,16},{1,9},{9,1},{17,25},{25,17},{2,10},{10... | collective-permute-start | bytes 589832 | tf_op jit(solution)/shard_map/ppermute | solution.py:418
  71.6 8.1 %collective-permute-start.1 = (f32[1,3,128,128]{3,2,1,0:T(8,128)S(1)}, f32[1,3,128,128]{3,2,1,0:T(8,128)S(1)}, u32[]{:S(2)}, u32[]{:S(2)}) collective-permute-start(f32[1,3,128,128]{3,2,1,0:T(8,128)S(1)} %get-tuple-element.24), channel_id=1, source_target_pairs={{8,16},{16,8},{24,0},{0,24},{9,17},{17,9},{25,1},{1,25},{10,18},{1... | collective-permute-start | bytes 589832 | tf_op jit(solution)/shard_map/ppermute | solution.py:418
  79.8 25.0 %collective-permute-start.2 = (f32[1,22,8,128]{3,2,1,0:T(8,128)S(1)}, f32[1,22,8,128]{3,2,1,0:T(8,128)S(1)}, u32[]{:S(2)}, u32[]{:S(2)}) collective-permute-start(f32[1,22,8,128]{3,2,1,0:T(8,128)S(1)} %get-tuple-element.25), channel_id=1, source_target_pairs={{0,1},{1,0},{2,3},{3,2},{4,5},{5,4},{6,7},{7,6},{8,9},{9,8},{10,11... | collective-permute-start | bytes 270344 | tf_op jit(solution)/shard_map/ppermute | solution.py:418
  79.9 24.9 %collective-permute-start.3 = (f32[1,22,8,128]{3,2,1,0:T(8,128)S(1)}, f32[1,22,8,128]{3,2,1,0:T(8,128)S(1)}, u32[]{:S(2)}, u32[]{:S(2)}) collective-permute-start(f32[1,22,8,128]{3,2,1,0:T(8,128)S(1)} %get-tuple-element.26), channel_id=1, source_target_pairs={{1,2},{2,1},{3,4},{4,3},{5,6},{6,5},{7,0},{0,7},{9,10},{10,9},{11,... | collective-permute-start | bytes 270344 | tf_op jit(solution)/shard_map/ppermute | solution.py:418
  127.0 0.7 copy-start.15
  127.7 19.4 %all-to-all-start.2 = ((f32[32,16,128]{2,1,0:T(8,128)}), f32[32,16,128]{2,1,0:T(8,128)S(1)}, u32[]{:S(2)}, u32[]{:S(2)}) async-start(f32[32,16,128]{2,1,0:T(8,128)} %copy-done.15), calls=%async_computation.2 | async-start | bytes 524288 | tf_op jit(solution)/shard_map/all_to_all | solution.py:526
  133.5 2.1 %copy-start.10 = (f32[2,24,152,128]{3,2,1,0:T(8,128)S(1)}, f32[2,24,152,128]{3,2,1,0:T(8,128)}, u32[]{:S(2)}) copy-start(f32[2,24,152,128]{3,2,1,0:T(8,128)} %get-tuple-element.39.v0_ref) | copy-start | bytes 11206660
  135.6 2.1 %copy-start.11 = (f32[2,24,152,128]{3,2,1,0:T(8,128)S(1)}, f32[2,24,152,128]{3,2,1,0:T(8,128)}, u32[]{:S(2)}) copy-start(f32[2,24,152,128]{3,2,1,0:T(8,128)} %get-tuple-element.40.v1_ref) | copy-start | bytes 11206660
  137.6 2.1 %copy-start.12 = (f32[2,24,152,128]{3,2,1,0:T(8,128)S(1)}, f32[2,24,152,128]{3,2,1,0:T(8,128)}, u32[]{:S(2)}) copy-start(f32[2,24,152,128]{3,2,1,0:T(8,128)} %get-tuple-element.41.v2_ref) | copy-start | bytes 11206660
  144.5 2.6 %copy-start = (f32[3,2,16,128,128]{4,3,2,1,0:T(8,128)}, f32[3,2,16,128,128]{4,3,2,1,0:T(8,128)S(1)}, u32[]{:S(2)}) copy-start(f32[3,2,16,128,128]{4,3,2,1,0:T(8,128)S(1)} %turn_back.1.v_ref) | copy-start | bytes 18874372
  147.1 2.8 %copy-start.1 = (f32[3,2,16,128,128]{4,3,2,1,0:T(8,128)S(1)}, f32[3,2,16,128,128]{4,3,2,1,0:T(8,128)}, u32[]{:S(2)}) copy-start(f32[3,2,16,128,128]{4,3,2,1,0:T(8,128)} %copy-done) | copy-start | bytes 18874372
where the time goes:
time: 153 us
  Pallas kernels  62 us (41%)
  waiting for transfers between devices  37.4 us (24%)
  starting transfers between devices  26.8 us (18%)
  local copies, waits for them, and re-layouts  25.6 us (17%)
    ppermute x8, waiting for transfers between devices, exchange(): return (lax.ppermute(a, axis, pair_a), lax.ppermute(b, axis, pair_b))  28.9 us
    unnamed x37, local copies, waits for them, and re-layouts  24.5 us
    pallas_call x1, Pallas kernels, shards(): pl.pallas_call(matrix_kernel, out_shape=(field,) * 6, in_specs=[VM] * 5 +...  23.4 us
    pallas_call x1, Pallas kernels, shards(): pl.pallas_call(krylov_kernel, out_shape=(field, field, field, shaped(32,...  22.2 us
    ppermute x8, starting transfers between devices, exchange(): return (lax.ppermute(a, axis, pair_a), lax.ppermute(b, axis, pair_b))  12.7 us
    all_to_all x1, waiting for transfers between devices, shards(): gathered = lax.all_to_all(absorbed, 'grp', 0, 0, tiled=True)  8.52 us
    all_to_all x1, starting transfers between devices, shards(): gathered = lax.all_to_all(absorbed, 'grp', 0, 0, tiled=True)  5.85 us
    pallas_call x1, Pallas kernels, shards(): pl.pallas_call(turn_back_kernel, out_shape=shaped(3, 2, NX, N, N), in_spe...  4.82 us
  transfers between devices with their start and end apart: 11, of which 4 were waited for; matrix products, arithmetic and copies ran while one was open for 1% of the time, Pallas kernels for 23%

commit v1 on v0

v1 whole, which is shorter than its diff:
```python
import functools

import jax
import jax.numpy as jnp
from jax import lax
from jax.experimental import pallas as pl
from jax.experimental.pallas import tpu as pltpu
from jax.sharding import PartitionSpec as P

DT = 0.5
SHIFT = 6.0
SCALE = 4.0
NX = 16
N = 128
MATS = 8
HE = 5
HT = 3
ROWS = 160
ZO = 16
PX = 24
CHUNKS = ((8, 48), (56, 48), (104, 48))
INNER = ((24, 48), (72, 48), (120, 16))
OUTER = ((8, 16), (136, 16))
OWN = ((16, 48), (64, 48), (112, 32))

SX_A = [(0, 1), (1, 0), (2, 3), (3, 2)]
SX_B = [(1, 2), (2, 1)]
SZ_A = [(0, 1), (1, 0), (2, 3), (3, 2), (4, 5), (5, 4), (6, 7), (7, 6)]
SZ_B = [(1, 2), (2, 1), (3, 4), (4, 3), (5, 6), (6, 5), (7, 0), (0, 7)]

VM = pl.BlockSpec(memory_space=pltpu.VMEM)
HB = pl.BlockSpec(memory_space=pltpu.HBM)
SM = pl.BlockSpec(memory_space=pltpu.SMEM)
F32 = jnp.float32


def shaped(*dims):
    return jax.ShapeDtypeStruct(dims, F32)


def in_vmem(value):
    return pltpu.with_memory_space_constraint(value, pltpu.VMEM)


def in_hbm(value):
    return pltpu.with_memory_space_constraint(value, pltpu.HBM)


def params(mib):
    return pltpu.CompilerParams(vmem_limit_bytes=mib * 1024 * 1024)


def cost(flops, nbytes):
    return pl.CostEstimate(flops=flops, bytes_accessed=nbytes, transcendentals=0)


def pick(species, values):
    b0, b1, b2 = ((species & k) != 0 for k in (1, 2, 4))
    level = [jnp.where(b0, values[2 * k + 1], values[2 * k]) for k in range(4)]
    level = [jnp.where(b1, level[1], level[0]), jnp.where(b1, level[3], level[2])]
    return jnp.where(b2, level[1], level[0])


def absorbed_kernel(e_ref, sp_ref, tab_ref, w_ref, out_ref):
    tabs = [[tab_ref[g, m] for m in range(MATS)] for g in range(2)]
    for k in range(2):
        rows = slice(k * 16, k * 16 + 16)
        for m in range(MATS):
            share = tabs[0][m] * w_ref[0] + tabs[1][m] * w_ref[1]
            out_ref[k, NX, m : m + 1, :] = jnp.full((1, N), share, F32)
        out_ref[k, NX, 8:16, :] = jnp.zeros((8, N), F32)
        for x in range(NX):
            species = sp_ref[x, rows, :]
            out_ref[k, x] = pick(species, tabs[0]) * e_ref[0, x, rows, :] + pick(species, tabs[1]) * e_ref[1, x, rows, :]


def pack_kernel(e_ref, sp_ref, a_ref, b_ref, e_buf, sp_buf, sem):
    even = lax.rem(lax.axis_index("sx"), 2) == 0

    def part(k, first):
        copies = [pltpu.make_async_copy(e_ref.at[g, pl.ds(first, HE)], e_buf.at[k, g], sem.at[k, g]) for g in range(2)]
        copies.append(pltpu.make_async_copy(sp_ref.at[pl.ds(first, HE)], sp_buf.at[k], sem.at[k, 2]))
        return copies

    both = [part(0, jnp.where(even, NX - HE, 0)), part(1, jnp.where(even, 0, NX - HE))]
    for copies in both:
        for copy in copies:
            copy.start()
    for k, out_ref in enumerate((a_ref, b_ref)):
        for copy in both[k]:
            copy.wait()
        for j in range(HE):
            for g in range(2):
                out_ref[g, j] = e_buf[k, g, j].T
            out_ref[2, j] = sp_buf[k, j].astype(F32).T


def turn_kernel(e_ref, sp_ref, out_ref):
    for x in range(4):
        for g in range(2):
            out_ref[g, x] = e_ref[g, x].T
        out_ref[2, x] = sp_ref[x].astype(F32).T


def side_kernel(own_ref, xa_ref, xb_ref, za_ref, zb_ref, sem):
    rows_a, rows_b = slice(0, 8), slice(N - 8, N)

    def send(low, high, first, last):
        copies = []
        for k, (out, rows) in enumerate(((first, rows_a), (last, rows_b))):
            for j, (ref, at, count) in enumerate(((low, 0, HE), (own_ref, HE, NX), (high, HE + NX, HE))):
                copies.append(pltpu.make_async_copy(ref.at[:, :, rows, :], out.at[:, at : at + count], sem.at[k, j]))
        for copy in copies:
            copy.start()
        for copy in copies:
            copy.wait()

    x_even = lax.rem(lax.axis_index("sx"), 2) == 0
    z_even = lax.rem(lax.axis_index("sz"), 2) == 0
    for x_is in (True, False):
        for z_is in (True, False):
            low, high = (xb_ref, xa_ref) if x_is else (xa_ref, xb_ref)
            first, last = (zb_ref, za_ref) if z_is else (za_ref, zb_ref)
            pl.when(jnp.logical_and(x_even == x_is, z_even == z_is))(
                functools.partial(send, low, high, first, last)
            )


def edge_rows(get, depth, a_ref, b_ref):
    even = lax.rem(lax.axis_index("sz"), 2) == 0
    to_a = pl.multiple_of(jnp.where(even, N - 8, 0), 8)
    to_b = pl.multiple_of(jnp.where(even, 0, N - 8), 8)
    for x in range(depth):
        a_ref[x] = get(x, to_a)
        b_ref[x] = get(x, to_b)


def corner_kernel(c_count, halo, own_ref, xa_ref, xb_ref, a_ref, b_ref):
    even = lax.rem(lax.axis_index("sx"), 2) == 0
    for c in range(c_count):

        def fill(low, high):
            def get(x, row):
                if x < halo:
                    return low[c, x, pl.ds(row, 8), :]
                if x < halo + NX:
                    return own_ref[c, x - halo, pl.ds(row, 8), :]
                return high[c, x - halo - NX, pl.ds(row, 8), :]

            edge_rows(get, NX + 2 * halo, a_ref.at[c], b_ref.at[c])

        pl.when(even)(lambda: fill(xb_ref, xa_ref))
        pl.when(jnp.logical_not(even))(lambda: fill(xa_ref, xb_ref))


def lanes(n):
    return lax.broadcasted_iota(jnp.int32, (n, N), 1)


def height(row, n):
    return lax.broadcasted_iota(jnp.int32, (n, N), 0) + (lax.axis_index("sz") * N + row - ZO)


def limiter_kernel(own_ref, xa_ref, xb_ref, za_ref, zb_ref, tab_ref, e_ref, d_ref, op_ref, spx_ref, sem):
    sx, sz = lax.axis_index("sx"), lax.axis_index("sz")
    tabs = [[tab_ref[g, m] for m in range(MATS)] for g in range(2)]
    below, middle, above = slice(ZO - 8, ZO), slice(ZO, ZO + N), slice(ZO + N, ZO + N + 8)
    x_even = lax.rem(sx, 2) == 0
    z_even = lax.rem(sz, 2) == 0

    def piece(c, ref, source, first, count, rows, k):
        planes = slice(first, first + count)
        target = spx_ref.at[planes, rows, :] if c == 2 else e_ref.at[c, planes, rows, :]
        return pltpu.make_async_copy(ref.at[c, source : source + count], target, sem.at[k, c])

    def start(low, high, x_low, x_high):
        for c in range(3):
            piece(c, x_low, 0, 0, HE, middle, 0).start()
            piece(c, low, 0, 0, NX + 2 * HE, below, 3).start()
            piece(c, high, 0, 0, NX + 2 * HE, above, 4).start()
            piece(c, own_ref, 0, HE, NX // 2, middle, 1).start()
            piece(c, own_ref, NX // 2, HE + NX // 2, NX // 2, middle, 2).start()
            piece(c, x_high, 0, HE + NX, HE, middle, 5).start()

    for x_is in (True, False):
        for z_is in (True, False):
            x_low, x_high = (xb_ref, xa_ref) if x_is else (xa_ref, xb_ref)
            low, high = (zb_ref, za_ref) if z_is else (za_ref, zb_ref)
            pl.when(jnp.logical_and(x_even == x_is, z_even == z_is))(
                functools.partial(start, low, high, x_low, x_high)
            )

    def finish(k, ref, source, first, count, rows):
        for c in range(3):
            piece(c, ref, source, first, count, rows, k).wait()

    finish(0, xa_ref, 0, 0, HE, middle)
    finish(3, za_ref, 0, 0, NX + 2 * HE, below)
    finish(4, za_ref, 0, 0, NX + 2 * HE, above)

    def clear(rows):
        def step(x, carry):
            for g in range(2):
                e_ref[g, x, rows, :] = jnp.zeros((8, N), F32)
            return carry

        lax.fori_loop(0, NX + 2 * HE, step, 0)

    pl.when(sz == 0)(lambda: clear(below))
    pl.when(sz == 7)(lambda: clear(above))
    finish(1, own_ref, 0, HE, NX // 2, middle)

    def coefficients(p, carry):
        pl.when(p == HE + NX // 2 - 2)(
            lambda: finish(2, own_ref, NX // 2, HE + NX // 2, NX // 2, middle)
        )
        pl.when(p == HE + NX - 2)(lambda: finish(5, xa_ref, 0, HE + NX, HE, middle))
        gx = sx * NX + p - 4
        x_in = jnp.logical_and(gx >= 0, gx < 4 * NX).astype(jnp.int32)
        for row, n in CHUNKS:
            gz = height(row, n)
            inside = jnp.logical_and(gz >= 0, gz < 8 * N * x_in)
            lane = lanes(n)
            rows = slice(row, row + n)
            species = spx_ref[p + 1, rows, :].astype(jnp.int32)
            for g in range(2):
                opacity = pick(species, tabs[g])
                center = e_ref[g, p + 1, rows, :]
                dx = e_ref[g, p + 2, rows, :] - e_ref[g, p, rows, :]
                dz = e_ref[g, p + 1, row + 1 : row + 1 + n, :] - e_ref[g, p + 1, row - 1 : row - 1 + n, :]
                above = jnp.where(lane == N - 1, 0.0, pltpu.roll(center, N - 1, 1))
                below = jnp.where(lane == 0, 0.0, pltpu.roll(center, 1, 1))
                dy = above - below
                square = 0.25 * (dx * dx + dy * dy + dz * dz)
                slope = jnp.sqrt(square)
                m = opacity * center
                upper = m * (2.0 * m + slope)
                lower = opacity * (m * (6.0 * m + 3.0 * slope) + square)
                d_ref[g, p, rows, :] = jnp.where(inside, upper / lower, 0.0)
                op_ref[g, p, rows, :] = opacity
        return carry

    lax.fori_loop(0, PX, coefficients, 0)


def operator_kernel(e_ref, d_ref, op_ref, w_ref, dg_ref, kx_ref, ky_ref, kz_ref, q_ref, ow_ref):
    sx = lax.axis_index("sx")
    inv = 1.0 / SCALE

    def operator(p, carry):
        gx = sx * NX + p - 4
        x_in = jnp.logical_and(gx >= 0, gx < 4 * NX).astype(jnp.int32)
        x_face = jnp.where(jnp.logical_and(gx >= 0, gx + 1 < 4 * NX), 0.5, 0.0)
        for row, n in CHUNKS:
            gz = height(row, n)
            inside = jnp.logical_and(gz >= 0, gz < 8 * N * x_in)
            z_face = jnp.where(jnp.logical_and(gz >= 0, gz + 1 < 8 * N), 0.5, 0.0)
            lane = lanes(n)
            rows = slice(row, row + n)
            up = slice(row + 1, row + 1 + n)
            down = slice(row - 1, row - 1 + n)
            for g in range(2):
                d = d_ref[g, p, rows, :]
                dxp, dxm = d_ref[g, p + 1, rows, :], d_ref[g, p - 1, rows, :]
                dzp, dzm = d_ref[g, p, up, :], d_ref[g, p, down, :]
                dyp = jnp.where(lane == N - 1, 0.0, pltpu.roll(d, N - 1, 1))
                dym = jnp.where(lane == 0, 0.0, pltpu.roll(d, 1, 1))
                opacity = op_ref[g, p, rows, :]
                sxp, sxm, szp, szm, syp, sym = (d + o for o in (dxp, dxm, dzp, dzm, dyp, dym))
                total = 0.5 * (((sxp + sxm) + (szp + szm)) + (syp + sym))
                diag = (1.0 / DT + opacity) + total
                center = e_ref[g, p + 1, rows, :]
                moved = (
                    (sxp * e_ref[g, p + 2, rows, :] + sxm * e_ref[g, p, rows, :])
                    + (szp * e_ref[g, p + 1, up, :] + szm * e_ref[g, p + 1, down, :])
                    + jnp.where(lane == N - 1, 0.0, syp * pltpu.roll(center, N - 1, 1))
                    + jnp.where(lane == 0, 0.0, sym * pltpu.roll(center, 1, 1))
                )
                q_ref[g, p, rows, :] = jnp.where(inside, (1.0 / DT - diag) * center + 0.5 * moved, 0.0)
                ow_ref[g, p, rows, :] = jnp.where(inside, opacity * w_ref[g], 0.0)
                dg_ref[g, p, rows, :] = jnp.where(inside, (diag - SHIFT) * inv, 0.0)
                kx_ref[g, p, rows, :] = sxp * (x_face * inv)
                kz_ref[g, p, rows, :] = szp * (z_face * inv)
                ky_ref[g, p, rows, :] = jnp.where(lane == N - 1, 0.0, syp * (0.5 * inv))
        return carry

    lax.fori_loop(1, PX - 1, operator, 0)


def temperature_kernel(g_ref, r_ref, t_ref, cap_ref, sp_ref, out_ref):
    shares = r_ref[0, NX, 0:8, :]
    for k in range(1, 8):
        shares = shares + r_ref[k, NX, 0:8, :]
    values = [jnp.broadcast_to(shares[m : m + 1, :], (16, N)) for m in range(MATS)]
    for x in range(NX):
        absorbed = r_ref[0, x]
        for k in range(1, 8):
            absorbed = absorbed + r_ref[k, x]
        t = t_ref[x]
        weight = pick(sp_ref[x], values)
        cube = t * t * t
        gain = absorbed - weight * (cube * t)
        slope = 4.0 * weight * cube
        after = t + DT * gain / (cap_ref[x] + DT * slope)
        for k in range(8):
            out_ref[k, x] = after


def emission_kernel(t_ref, out_ref, a_ref, b_ref, after_ref):
    for x in range(NX):
        t = t_ref[:, x].reshape(N, N)
        after_ref[x] = t
        square = t * t
        out_ref[0, x] = (square * square).T
    even = lax.rem(lax.axis_index("sx"), 2) == 0
    to_a = jnp.where(even, NX - HT, 0)
    to_b = jnp.where(even, 0, NX - HT)
    for j in range(HT):
        a_ref[0, j] = out_ref[0, to_a + j]
        b_ref[0, j] = out_ref[0, to_b + j]


def applied(v_ref, dg_ref, kx_ref, ky_ref, kz_ref, g, p, row, n):
    rows = slice(row, row + n)
    up = slice(row + 1, row + 1 + n)
    down = slice(row - 1, row - 1 + n)
    c = v_ref[g, p, rows, :]
    ky = ky_ref[g, p, rows, :]
    total = dg_ref[g, p, rows, :] * c
    total = total - kx_ref[g, p, rows, :] * v_ref[g, p + 1, rows, :]
    total = total - kx_ref[g, p - 1, rows, :] * v_ref[g, p - 1, rows, :]
    total = total - kz_ref[g, p, rows, :] * v_ref[g, p, up, :]
    total = total - kz_ref[g, p, down, :] * v_ref[g, p, down, :]
    total = total - ky * pltpu.roll(c, N - 1, 1)
    return total - pltpu.roll(ky * c, 1, 1)


def inner_kernel(
    own_ref, xa_ref, xb_ref, dg_ref, kx_ref, ky_ref, kz_ref, q_ref, ow_ref, v0_ref, v1_ref
):
    def first(plane, ref, count):
        def step(j, carry):
            p = plane + j
            for row, n in OWN:
                rows = slice(row, row + n)
                t = ref[0, j, row - ZO : row - ZO + n, :]
                for g in range(2):
                    v0_ref[g, p, rows, :] = q_ref[g, p, rows, :] + ow_ref[g, p, rows, :] * t
            return carry

        lax.fori_loop(0, count, step, 0)

    even = lax.rem(lax.axis_index("sx"), 2) == 0

    def sides(low, high):
        first(4 - HT, low, HT)
        first(4 + NX, high, HT)

    pl.when(even)(lambda: sides(xb_ref, xa_ref))
    pl.when(jnp.logical_not(even))(lambda: sides(xa_ref, xb_ref))
    first(4, own_ref, NX)

    def second(p, carry):
        for g in range(2):
            for row, n in INNER:
                v1_ref[g, p, row : row + n, :] = applied(v0_ref, dg_ref, kx_ref, ky_ref, kz_ref, g, p, row, n)
        return carry

    lax.fori_loop(2, PX - 2, second, 0)


def krylov_kernel(
    za_ref, zb_ref, dg_ref, kx_ref, ky_ref, kz_ref, v0_in, v1_in, ow_ref,
    v0_ref, v1_ref, v2_ref, mom_ref,
):
    apply = functools.partial(applied, dg_ref=dg_ref, kx_ref=kx_ref, ky_ref=ky_ref, kz_ref=kz_ref)

    def edges(low, high):
        def step(p, carry):
            for g in range(2):
                for row, t in ((ZO - 4, low[0, p - 1, 4:8, :]), (ZO + N, high[0, p - 1, 0:4, :])):
                    rows = slice(row, row + 4)
                    v0_ref[g, p, rows, :] = v0_ref[g, p, rows, :] + ow_ref[g, p, rows, :] * t
            return carry

        lax.fori_loop(1, PX - 1, step, 0)

    z_even = lax.rem(lax.axis_index("sz"), 2) == 0
    pl.when(z_even)(lambda: edges(zb_ref, za_ref))
    pl.when(jnp.logical_not(z_even))(lambda: edges(za_ref, zb_ref))

    for source, target, start, chunks in ((v0_ref, v1_ref, 2, OUTER), (v1_ref, v2_ref, 3, CHUNKS)):

        def step(p, carry, source=source, target=target, chunks=chunks):
            for g in range(2):
                for row, n in chunks:
                    target[g, p, row : row + n, :] = apply(source, g=g, p=p, row=row, n=n)
            return carry

        lax.fori_loop(start, PX - start, step, 0)

    def fold(value):
        return jnp.sum(value.reshape(-1, 8, N), axis=0)

    for g in range(2):

        def last(p, sums, g=g):
            sums = list(sums)
            for row, n in OWN:
                rows = slice(row, row + n)
                a, b, c = v0_ref[g, p, rows, :], v1_ref[g, p, rows, :], v2_ref[g, p, rows, :]
                d = apply(v2_ref, g=g, p=p, row=row, n=n)
                for k, (l, r) in enumerate(((a, a), (a, b), (b, b), (b, c), (c, c), (c, d))):
                    sums[k] = sums[k] + fold(l * r)
            return tuple(sums)

        sums = lax.fori_loop(4, 4 + NX, last, (jnp.zeros((8, N), F32),) * 6)
        for k in range(6):
            line = jnp.sum(sums[k], axis=0, keepdims=True)
            for peer in range(mom_ref.shape[0]):
                mom_ref[peer, g * 8 + k : g * 8 + k + 1, :] = line
        for peer in range(mom_ref.shape[0]):
            mom_ref[peer, g * 8 + 6 : g * 8 + 8, :] = jnp.zeros((2, N), F32)


def update_kernel(mom_ref, e_ref, v0_ref, v1_ref, v2_ref, out_ref, c_ref):
    @pl.when(pl.program_id(0) == 0)
    def _():
        total = mom_ref[0]
        for k in range(1, mom_ref.shape[0]):
            total = total + mom_ref[k]
        total = jnp.sum(total, axis=1, keepdims=True)
        for g in range(2):
            n = [total[g * 8 + k : g * 8 + k + 1, :] for k in range(6)]
            m = [SHIFT * n[k] + SCALE * n[k + 1] for k in range(5)]
            l1 = m[1] / m[0]
            l2 = m[2] / m[0]
            p1 = m[2] - l1 * m[1]
            u = m[3] - l1 * m[2]
            r1 = n[1] - l1 * n[0]
            ok1 = p1 > 1e-6 * m[2]
            s1 = jnp.where(ok1, u / p1, 0.0)
            p2 = m[4] - l2 * m[2] - s1 * u
            r2 = n[2] - l2 * n[0] - s1 * r1
            ok2 = jnp.logical_and(ok1, p2 > 1e-6 * m[4])
            c2 = jnp.where(ok2, r2 / p2, 0.0)
            c1 = jnp.where(ok1, (r1 - u * c2) / p1, 0.0)
            c0 = (n[0] - m[1] * c1 - m[2] * c2) / m[0]
            for k, c in enumerate((c0, c1, c2)):
                c_ref[g * 3 + k] = jnp.broadcast_to(c, (8, N))

    rows = slice(ZO, ZO + N)
    for x in range(4):
        p = pl.program_id(0) * 4 + (x + 4)
        for g in range(2):
            total = v0_ref[g, p, rows, :] * c_ref[g * 3, 0:1, :]
            total = total + v1_ref[g, p, rows, :] * c_ref[g * 3 + 1, 0:1, :]
            total = total + v2_ref[g, p, rows, :] * c_ref[g * 3 + 2, 0:1, :]
            out_ref[g, x] = e_ref[g, x] + total.T


def exchange(a, b, axis, pair_a, pair_b):
    return lax.ppermute(a, axis, pair_a), lax.ppermute(b, axis, pair_b)


def shards(energy, kelvin, capacity, species, table, fraction):
    table = table.T
    planes = lambda k: pl.BlockSpec((2, k, N, N), lambda i: (0, i, 0, 0))
    single = lambda k: pl.BlockSpec((k, N, N), lambda i: (i, 0, 0))
    whole = lambda *d: pl.BlockSpec(d, lambda *_: (0,) * len(d))

    absorbed = pl.pallas_call(
        absorbed_kernel,
        out_shape=shaped(8, NX + 1, 16, N),
        grid=(4,),
        in_specs=[
            pl.BlockSpec((2, NX, 32, N), lambda i: (0, 0, i, 0)),
            pl.BlockSpec((NX, 32, N), lambda i: (0, i, 0)),
            SM,
            SM,
        ],
        out_specs=pl.BlockSpec((2, NX + 1, 16, N), lambda i: (i, 0, 0, 0)),
        compiler_params=params(60),
        cost_estimate=cost(10_000_000, 4_000_000),
        name="absorbed",
    )(energy, species, table, fraction)
    gathered = lax.all_to_all(absorbed, "grp", 0, 0, tiled=True)

    field = pltpu.VMEM((2, PX, ROWS, N), F32)
    wide = pltpu.VMEM((2, NX + 2 * HE, ROWS, N), F32)
    xa, xb = pl.pallas_call(
        pack_kernel,
        out_shape=(pltpu.HBM((3, HE, N, N), F32),) * 2,
        in_specs=[HB, HB],
        out_specs=(VM, VM),
        scratch_shapes=[
            pltpu.VMEM((2, 2, HE, N, N), F32),
            pltpu.VMEM((2, HE, N, N), jnp.int32),
            pltpu.SemaphoreType.DMA((2, 3)),
        ],
        compiler_params=params(6),
        cost_estimate=cost(1_000_000, 4_000_000),
        name="pack",
    )(in_hbm(energy), in_hbm(species))
    xa, xb = map(in_vmem, exchange(xa, xb, "sx", SX_A, SX_B))
    own = pl.pallas_call(
        turn_kernel,
        out_shape=pltpu.HBM((3, NX, N, N), F32),
        grid=(4,),
        in_specs=[planes(4), single(4)],
        out_specs=pl.BlockSpec((3, 4, N, N), lambda i: (0, i, 0, 0)),
        compiler_params=params(8),
        cost_estimate=cost(10_000_000, 8_000_000),
        name="turn",
    )(in_hbm(energy), in_hbm(species))
    gathered, own = lax.optimization_barrier((gathered, own))
    za, zb = pl.pallas_call(
        side_kernel,
        out_shape=(pltpu.HBM((3, NX + 2 * HE, 8, N), F32),) * 2,
        in_specs=[HB, VM, VM],
        out_specs=(VM,) * 2,
        scratch_shapes=[pltpu.SemaphoreType.DMA((2, 3))],
        compiler_params=params(2),
        cost_estimate=cost(1000, 1_000_000),
        name="sides",
    )(in_hbm(own), xa, xb)
    za, zb = map(in_vmem, exchange(za, zb, "sz", SZ_A, SZ_B))
    ext, diffusion, opacity = pl.pallas_call(
        limiter_kernel,
        out_shape=(wide, field, field),
        in_specs=[HB] + [VM] * 4 + [SM],
        out_specs=(VM,) * 3,
        scratch_shapes=[
            pltpu.VMEM((NX + 2 * HE, ROWS, N), F32),
            pltpu.SemaphoreType.DMA((6, 3)),
        ],
        compiler_params=params(5),
        cost_estimate=cost(100_000_000, 15_000_000),
        name="limiter",
    )(in_hbm(own), xa, xb, za, zb, table)
    share = pl.BlockSpec((NX, 16, N), lambda i, g: (0, g[0], 0))
    where = lax.axis_index("grp").astype(jnp.int32).reshape(1)
    after = pl.pallas_call(
        temperature_kernel,
        out_shape=pltpu.HBM((8, NX, 16, N), F32),
        grid_spec=pltpu.PrefetchScalarGridSpec(
            num_scalar_prefetch=1,
            grid=(1,),
            in_specs=[VM, share, share, share],
            out_specs=whole(8, NX, 16, N),
        ),
        compiler_params=params(8),
        cost_estimate=cost(1_000_000, 3_000_000),
        name="temperature",
    )(where, gathered, in_hbm(kelvin), in_hbm(capacity), in_hbm(species))
    after = lax.all_to_all(after, "grp", 0, 0, tiled=True)

    own_t, ta, tb, kelvin_after = pl.pallas_call(
        emission_kernel,
        out_shape=(shaped(1, NX, N, N), shaped(1, HT, N, N), shaped(1, HT, N, N), shaped(NX, N, N)),
        in_specs=[VM],
        out_specs=(VM,) * 4,
        compiler_params=params(6),
        cost_estimate=cost(1_000_000, 3_000_000),
        name="emission",
    )(after)
    ta, tb = exchange(ta, tb, "sx", SX_A, SX_B)
    own_t, diffusion = lax.optimization_barrier((own_t, diffusion))
    tza, tzb = pl.pallas_call(
        functools.partial(corner_kernel, 1, HT),
        out_shape=(shaped(1, NX + 2 * HT, 8, N),) * 2,
        in_specs=[VM] * 3,
        out_specs=(VM, VM),
        compiler_params=params(9),
        cost_estimate=cost(1000, 300_000),
        name="corners_t",
    )(own_t, ta, tb)
    tza, tzb = exchange(tza, tzb, "sz", SZ_A, SZ_B)

    *coefs, q, emit = pl.pallas_call(
        operator_kernel,
        out_shape=(field,) * 6,
        in_specs=[VM] * 3 + [SM],
        out_specs=(VM,) * 6,
        input_output_aliases={2: 5},
        compiler_params=params(4),
        cost_estimate=cost(100_000_000, 15_000_000),
        name="operator",
    )(in_vmem(ext), in_vmem(diffusion), in_vmem(opacity), fraction)

    v0, v1 = pl.pallas_call(
        inner_kernel,
        out_shape=(field, field),
        in_specs=[VM] * 9,
        out_specs=(VM,) * 2,
        input_output_aliases={7: 0},
        compiler_params=params(4),
        cost_estimate=cost(50_000_000, 10_000_000),
        name="inner",
    )(own_t, ta, tb, *map(in_vmem, (*coefs, q, emit)))
    v0, v1, v2, mom = pl.pallas_call(
        krylov_kernel,
        out_shape=(field, field, field, pltpu.HBM((32, 16, N), F32)),
        in_specs=[VM] * 9,
        out_specs=(VM,) * 4,
        input_output_aliases={6: 0, 7: 1, 8: 2},
        compiler_params=params(4),
        cost_estimate=cost(100_000_000, 30_000_000),
        name="krylov",
    )(tza, tzb, *map(in_vmem, (*coefs, v0, v1, emit)))
    mom = lax.all_to_all(mom, ("sx", "sz"), 0, 0, tiled=True)
    result = pl.pallas_call(
        update_kernel,
        out_shape=shaped(2, NX, N, N),
        grid=(4,),
        in_specs=[
            whole(32, 16, N),
            planes(4),
            VM,
            VM,
            VM,
        ],
        out_specs=planes(4),
        scratch_shapes=[pltpu.VMEM((6, 8, N), F32)],
        compiler_params=params(16),
        cost_estimate=cost(10_000_000, 10_000_000),
        name="update",
    )(mom, energy, in_vmem(v0), in_vmem(v1), in_vmem(v2))
    return result, kelvin_after


def solution(mesh):
    placed = (
        P("grp", "sx", None, "sz"),
        P("sx", None, "sz"),
        P("sx", None, "sz"),
        P("sx", None, "sz"),
        P(None, "grp"),
        P("grp"),
    )
    return jax.shard_map(
        shards,
        mesh=mesh,
        in_specs=placed,
        out_specs=(P("grp", "sx", None, "sz"), P("sx", None, "sz")),
        check_vma=False,
    )
```

time: 153 us -> 109 us (0.71)
  waiting for transfers between devices: 37.4 us -> 11.1 us
  local copies, waits for them, and re-layouts: 25.6 us -> 0.01 us
  blocking collectives: 0 us -> 17.1 us
  Pallas kernels: 62 us -> 46.8 us
  starting transfers between devices: 26.8 us -> 33 us
    unnamed x37 -> x6, local copies, waits for them, and re-layouts: 24.5 us -> 0.01 us
    ppermute x8, waiting for transfers between devices: 28.9 us -> 4.97 us  [exchange(): return (lax.ppermute(a, axis, pair_a), lax.ppermute(b, axis, pair_b))]
    pallas_call x6 -> x8, Pallas kernels: 57.3 us -> 38.9 us  [the longest x1 8.96 us: shards(): pl.pallas_call(krylov_kernel, out_shape=(field, field, field, pltpu.HBM((...]
    all_to_all x0 -> x1, blocking collectives: none -> 17.1 us  [shards(): mom = lax.all_to_all(mom, ('sx', 'sz'), 0, 0, tiled=True)]
    ppermute x8, starting transfers between devices: 12.7 us -> 23.4 us  [exchange(): return (lax.ppermute(a, axis, pair_a), lax.ppermute(b, axis, pair_b))]
    all_to_all x1, waiting for transfers between devices: 8.52 us -> 3.62 us  [shards(): gathered = lax.all_to_all(absorbed, 'grp', 0, 0, tiled=True)]
    all_to_all x1 -> x0, starting transfers between devices: 4.69 us -> none  [shards(): mom = lax.all_to_all(mom, ('sx', 'sz'), 0, 0, tiled=True)]
    all_to_all x1, waiting for transfers between devices: 0.01 us -> 2.51 us  [shards(): after = lax.all_to_all(after, 'grp', 0, 0, tiled=True)]
  transfers between devices with their start and end apart: 11 -> 10, of which waited for: 4 -> 3; matrix products, arithmetic and copies ran while one was open for 1% -> 0% of each run, Pallas kernels for 23% -> 29%
where the time goes in v1:
time: 109 us
  Pallas kernels  46.8 us (43%)
  starting transfers between devices  33 us (30%)
  blocking collectives  17.1 us (16%)
  waiting for transfers between devices  11.1 us (10%)
    ppermute x8, starting transfers between devices, exchange(): return (lax.ppermute(a, axis, pair_a), lax.ppermute(b, axis, pair_b))  23.4 us
    all_to_all x1, blocking collectives, shards(): mom = lax.all_to_all(mom, ('sx', 'sz'), 0, 0, tiled=True)  17.1 us
    pallas_call x1, Pallas kernels, shards(): pl.pallas_call(krylov_kernel, out_shape=(field, field, field, pltpu.HBM((...  8.96 us
    pallas_call x1, Pallas kernels, shards(): pl.pallas_call(limiter_kernel, out_shape=(wide, field, field), in_specs=[...  8.75 us
    pallas_call x1, Pallas kernels, shards(): pl.pallas_call(operator_kernel, out_shape=(field,) * 6, in_specs=[VM] * 3...  6.36 us
    all_to_all x1, starting transfers between devices, shards(): gathered = lax.all_to_all(absorbed, 'grp', 0, 0, tiled=True)  5.85 us
    ppermute x8, waiting for transfers between devices, exchange(): return (lax.ppermute(a, axis, pair_a), lax.ppermute(b, axis, pair_b))  4.97 us
    pallas_call x1, Pallas kernels, shards(): pl.pallas_call(turn_kernel, out_shape=pltpu.HBM((3, NX, N, N), F32), grid...  4.61 us
  transfers between devices with their start and end apart: 10, of which 3 were waited for; matrix products, arithmetic and copies ran while one was open for 0% of the time, Pallas kernels for 29%

profile of v1, /device:TPU:1, one launch (start us, length us, event | category | flops | bytes accessed | tf_op | source)
XLA Modules:
  0.0 108.8 jit_solution(2910558658297669389)
XLA Ops:
  0.6 4.2 %absorbed.1 = f32[8,17,16,128]{3,2,1,0:T(8,128)} custom-call(f32[2,16,128,128]{3,2,1,0:T(8,128)} %e_ref.7, s32[16,128,128]{2,1,0:T(8,128)} %sp_ref.7, f32[2,8]{1,0:T(2,128)} %bitcast.2, f32[2]{0:T(128)} %w_ref.3), custom_call_target="tpu_custom_call" | custom-call | flops 10000000 | bytes 4000000 | tf_op jit(solution)/shard_map/absorbed/pallas_call | solution.py:472
  4.8 5.9 %all-to-all-start = ((f32[8,17,16,128]{3,2,1,0:T(8,128)}), f32[8,17,16,128]{3,2,1,0:T(8,128)S(1)}, u32[]{:S(2)}, u32[]{:S(2)}) async-start(f32[8,17,16,128]{3,2,1,0:T(8,128)} %absorbed.1), calls=%async_computation | async-start | bytes 2228224 | tf_op jit(solution)/shard_map/all_to_all | solution.py:487
  10.6 2.9 %pack.1 = (f32[3,5,128,128]{3,2,1,0:T(8,128)}, f32[3,5,128,128]{3,2,1,0:T(8,128)}) custom-call(f32[2,16,128,128]{3,2,1,0:T(8,128)} %e_ref.7, s32[16,128,128]{2,1,0:T(8,128)} %sp_ref.7), custom_call_target="tpu_custom_call" | custom-call | flops 1000000 | bytes 4000000 | tf_op jit(solution)/shard_map/pack/pallas_call | solution.py:491
  13.5 1.0 collective-permute-start
  14.6 4.4 %collective-permute-start.1 = (f32[3,5,128,128]{3,2,1,0:T(8,128)}, f32[3,5,128,128]{3,2,1,0:T(8,128)S(1)}, u32[]{:S(2)}, u32[]{:S(2)}) collective-permute-start(f32[3,5,128,128]{3,2,1,0:T(8,128)} %get-tuple-element.35), channel_id=1, source_target_pairs={{8,16},{16,8},{9,17},{17,9},{10,18},{18,10},{11,19},{19,11},{12,20... | collective-permute-start | bytes 2949128 | tf_op jit(solution)/shard_map/ppermute | solution.py:463
  19.0 4.6 %turn.1.own_ref = f32[3,16,128,128]{3,2,1,0:T(8,128)} custom-call(f32[2,16,128,128]{3,2,1,0:T(8,128)} %e_ref.7, s32[16,128,128]{2,1,0:T(8,128)} %sp_ref.7), custom_call_target="tpu_custom_call" | custom-call | flops 10000000 | bytes 8000000 | tf_op jit(solution)/shard_map/turn/pallas_call | solution.py:506
  23.6 3.6 %all-to-all-done.r_ref = f32[8,17,16,128]{3,2,1,0:T(8,128)S(1)} async-done(((f32[8,17,16,128]{3,2,1,0:T(8,128)}), f32[8,17,16,128]{3,2,1,0:T(8,128)S(1)}, u32[]{:S(2)}, u32[]{:S(2)}) %all-to-all-start) | async-done | bytes 1114144 | tf_op jit(solution)/shard_map/all_to_all | solution.py:487
  27.2 2.2 %temperature.1 = f32[8,16,16,128]{3,2,1,0:T(8,128)} custom-call(s32[1]{0:T(128)} %bitcast.g_ref, f32[8,17,16,128]{3,2,1,0:T(8,128)S(1)} %all-to-all-done.r_ref, f32[16,128,128]{2,1,0:T(8,128)} %t_ref.1, f32[16,128,128]{2,1,0:T(8,128)} %cap_ref.1, s32[16,128,128]{2,1,0:T(8,128)} %sp_ref.7), custom_call_target="tpu_custom_call" | custom-call | flops 1000000 | bytes 3000000 | tf_op jit(solution)/shard_map/temperature/pallas_call | solution.py:543
  29.4 0.0 copy-start.1
  29.4 3.7 %all-to-all-start.1 = ((f32[8,16,16,128]{3,2,1,0:T(8,128)}), f32[8,16,16,128]{3,2,1,0:T(8,128)S(1)}, u32[]{:S(2)}, u32[]{:S(2)}) async-start(f32[8,16,16,128]{3,2,1,0:T(8,128)} %temperature.1), calls=%async_computation.1 | async-start | bytes 2097152 | tf_op jit(solution)/shard_map/all_to_all | solution.py:556
  33.1 0.0 collective-permute-done.xa_ref
  33.1 5.0 %collective-permute-done.1.xb_ref = f32[3,5,128,128]{3,2,1,0:T(8,128)S(1)} collective-permute-done((f32[3,5,128,128]{3,2,1,0:T(8,128)}, f32[3,5,128,128]{3,2,1,0:T(8,128)S(1)}, u32[]{:S(2)}, u32[]{:S(2)}) %collective-permute-start.1) | collective-permute-done | bytes 983072 | tf_op jit(solution)/shard_map/ppermute | solution.py:463
  38.1 1.9 %sides.1 = (f32[3,26,8,128]{3,2,1,0:T(8,128)}, f32[3,26,8,128]{3,2,1,0:T(8,128)}) custom-call(f32[3,16,128,128]{3,2,1,0:T(8,128)} %turn.1.own_ref, f32[3,5,128,128]{3,2,1,0:T(8,128)S(1)} %collective-permute-done.xa_ref, f32[3,5,128,128]{3,2,1,0:T(8,128)S(1)} %collective-permute-done.1.xb_ref), custom_call_target="tpu_custom_call" | custom-call | flops 1000 | bytes 1000000 | tf_op jit(solution)/shard_map/sides/pallas_call | solution.py:517
  40.0 1.7 %collective-permute-start.2 = (f32[3,26,8,128]{3,2,1,0:T(8,128)}, f32[3,26,8,128]{3,2,1,0:T(8,128)S(1)}, u32[]{:S(2)}, u32[]{:S(2)}) collective-permute-start(f32[3,26,8,128]{3,2,1,0:T(8,128)} %get-tuple-element.36), channel_id=1, source_target_pairs={{0,1},{1,0},{2,3},{3,2},{4,5},{5,4},{6,7},{7,6},{8,9},{9,8},{10,11... | collective-permute-start | bytes 958472 | tf_op jit(solution)/shard_map/ppermute | solution.py:463
  41.7 0.0 copy-start.2
  41.7 4.7 %collective-permute-start.3 = (f32[3,26,8,128]{3,2,1,0:T(8,128)}, f32[3,26,8,128]{3,2,1,0:T(8,128)}, u32[]{:S(2)}, u32[]{:S(2)}) collective-permute-start(f32[3,26,8,128]{3,2,1,0:T(8,128)} %get-tuple-element.37), channel_id=1, source_target_pairs={{1,2},{2,1},{3,4},{4,3},{5,6},{6,5},{7,0},{0,7},{9,10},{10,9},{11,... | collective-permute-start | bytes 958472 | tf_op jit(solution)/shard_map/ppermute | solution.py:463
  46.4 2.5 %all-to-all-done.1.t_ref = f32[8,16,16,128]{3,2,1,0:T(8,128)S(1)} async-done(((f32[8,16,16,128]{3,2,1,0:T(8,128)}), f32[8,16,16,128]{3,2,1,0:T(8,128)S(1)}, u32[]{:S(2)}, u32[]{:S(2)}) %all-to-all-start.1) | async-done | bytes 1048608 | tf_op jit(solution)/shard_map/all_to_all | solution.py:556
  48.9 1.2 %emission.1 = (f32[1,16,128,128]{3,2,1,0:T(8,128)S(1)}, f32[1,3,128,128]{3,2,1,0:T(8,128)S(1)}, f32[1,3,128,128]{3,2,1,0:T(8,128)S(1)}, f32[16,128,128]{2,1,0:T(8,128)}) custom-call(f32[8,16,16,128]{3,2,1,0:T(8,128)S(1)} %all-to-all-done.1.t_ref), custom_call_target="tpu_custom_call" | custom-call | flops 1000000 | bytes 3000000 | tf_op jit(solution)/shard_map/emission/pallas_call | solution.py:558
  50.1 0.8 collective-permute-start.4
  50.9 4.4 %collective-permute-start.5 = (f32[1,3,128,128]{3,2,1,0:T(8,128)S(1)}, f32[1,3,128,128]{3,2,1,0:T(8,128)S(1)}, u32[]{:S(2)}, u32[]{:S(2)}) collective-permute-start(f32[1,3,128,128]{3,2,1,0:T(8,128)S(1)} %get-tuple-element.41), channel_id=1, source_target_pairs={{8,16},{16,8},{9,17},{17,9},{10,18},{18,10},{11,19},{19,11},{12,20... | collective-permute-start | bytes 589832 | tf_op jit(solution)/shard_map/ppermute | solution.py:463
  55.3 0.0 collective-permute-done.2.za_ref
  55.3 0.0 collective-permute-done.3.zb_ref
  55.3 0.0 copy-done.1
  55.3 8.8 %limiter.1 = (f32[2,26,160,128]{3,2,1,0:T(8,128)S(1)}, f32[2,24,160,128]{3,2,1,0:T(8,128)S(1)}, f32[2,24,160,128]{3,2,1,0:T(8,128)S(1)}) custom-call(f32[3,16,128,128]{3,2,1,0:T(8,128)} %turn.1.own_ref, f32[3,5,128,128]{3,2,1,0:T(8,128)S(1)} %collective-permute-done.xa_ref, f32[3,5,128,128]{3,2,1,0:T(8,128)S(1)} %collective-permute-done.1.xb_ref, ...), custom_call_target="tpu_custom_call" | custom-call | flops 100000000 | bytes 15000000 | tf_op jit(solution)/shard_map/limiter/pallas_call | solution.py:528
  64.1 0.0 collective-permute-done.4.xa_ref
  64.1 0.0 collective-permute-done.5.xb_ref
  64.1 0.1 corners_t.1
  64.2 1.7 %collective-permute-start.6 = (f32[1,22,8,128]{3,2,1,0:T(8,128)S(1)}, f32[1,22,8,128]{3,2,1,0:T(8,128)S(1)}, u32[]{:S(2)}, u32[]{:S(2)}) collective-permute-start(f32[1,22,8,128]{3,2,1,0:T(8,128)S(1)} %get-tuple-element.42), channel_id=1, source_target_pairs={{0,1},{1,0},{2,3},{3,2},{4,5},{5,4},{6,7},{7,6},{8,9},{9,8},{10,11... | collective-permute-start | bytes 270344 | tf_op jit(solution)/shard_map/ppermute | solution.py:463
  65.9 4.7 %collective-permute-start.7 = (f32[1,22,8,128]{3,2,1,0:T(8,128)S(1)}, f32[1,22,8,128]{3,2,1,0:T(8,128)S(1)}, u32[]{:S(2)}, u32[]{:S(2)}) collective-permute-start(f32[1,22,8,128]{3,2,1,0:T(8,128)S(1)} %get-tuple-element.43), channel_id=1, source_target_pairs={{1,2},{2,1},{3,4},{4,3},{5,6},{6,5},{7,0},{0,7},{9,10},{10,9},{11,... | collective-permute-start | bytes 270344 | tf_op jit(solution)/shard_map/ppermute | solution.py:463
  70.6 0.0 copy-done.2
  70.6 6.4 %operator.1 = (f32[2,24,160,128]{3,2,1,0:T(8,128)S(1)}, f32[2,24,160,128]{3,2,1,0:T(8,128)S(1)}, f32[2,24,160,128]{3,2,1,0:T(8,128)S(1)}, f32[2,24,160,128]{3,2,...) custom-call(f32[2,26,160,128]{3,2,1,0:T(8,128)S(1)} %get-tuple-eleme, ...), custom_call_target="tpu_custom_call", output_to_operand_aliasing={{5}: (2, {})} | custom-call | flops 100000000 | bytes 15000000 | tf_op jit(solution)/shard_map/operator/pallas_call | solution.py:580
  76.9 3.2 %inner.1 = (f32[2,24,160,128]{3,2,1,0:T(8,128)S(1)}, f32[2,24,160,128]{3,2,1,0:T(8,128)S(1)}) custom-call(f32[1,16,128,128]{3,2,1,0:T(8,128)S(1)} %get-tuple-element.39.own_ref, f32[1,3,128,128]{3,2,1,0:T(8,128)S(1)} %collective-permute-done.4.xa_ref, f32[1,3,128,128]{3,2,1,0:T(8,128)S(1)} %collective-permute-done.5.xb_ref, ...), custom_call_target="tpu_custom_call", output_to_operand_aliasing={{0}: (7, {})} | custom-call | flops 50000000 | bytes 10000000 | tf_op jit(solution)/shard_map/inner/pallas_call | solution.py:591
  80.1 0.0 collective-permute-done.6.za_ref
  80.2 0.0 collective-permute-done.7.zb_ref
  80.2 0.0 copy-start
  80.2 9.0 %krylov.1 = (f32[2,24,160,128]{3,2,1,0:T(8,128)S(1)}, f32[2,24,160,128]{3,2,1,0:T(8,128)S(1)}, f32[2,24,160,128]{3,2,1,0:T(8,128)S(1)}, f32[32,16,128]{2,1,0:T(8,128)}) custom-call(f32[1,22,8,128]{3,2,1,0:T(8,128)S(1)} %collective-permute-done.6.za_ref, ...), custom_call_target="tpu_custom_call", output_to_operand_aliasing={{0}: (6, {}), {1}: (7, {}), {2}: (8, {})} | custom-call | flops 100000000 | bytes 30000000 | tf_op jit(solution)/shard_map/krylov/pallas_call | solution.py:601
  89.1 17.1 %all_to_all.15.mom_ref = f32[32,16,128]{2,1,0:T(8,128)S(1)} all-to-all(f32[32,16,128]{2,1,0:T(8,128)} %get-tuple-element.55), channel_id=1, replica_groups=mesh['grp'=8,'sx'=4,'sz'=8] {'sx','sz'}, dimensions={0} | all-to-all | bytes 524288 | tf_op jit(solution)/shard_map/all_to_all | solution.py:611
  106.3 0.0 copy-done
  106.3 2.6 %update.1 = f32[2,16,128,128]{3,2,1,0:T(8,128)} custom-call(f32[32,16,128]{2,1,0:T(8,128)S(1)} %all_to_all.15.mom_ref, f32[2,16,128,128]{3,2,1,0:T(8,128)S(1)} %copy-done, f32[2,24,160,128]{3,2,1,0:T(8,128)S(1)} %get-tuple-element.56.v0_ref, f32[2,24,160,128]{3,2,1,0:T(8,128)S(1)} %get-tuple-element.57.v1_ref, f32[2,24,160,128]{3,2,1,0:T(8,128)S(1)} %get-tuple-element.58.v2_ref), custom_call_target="tpu_custom_call" | custom-call | flops 10000000 | bytes 10000000 | tf_op jit(solution)/shard_map/update/pallas_call | solution.py:612
Async XLA Ops:
  4.8 22.5 %all-to-all-start = ((f32[8,17,16,128]{3,2,1,0:T(8,128)}), f32[8,17,16,128]{3,2,1,0:T(8,128)S(1)}, u32[]{:S(2)}, u32[]{:S(2)}) async-start(f32[8,17,16,128]{3,2,1,0:T(8,128)} %absorbed.1), calls=%async_computation | async-start | bytes 2228224 | tf_op jit(solution)/shard_map/all_to_all | solution.py:487
  13.5 19.6 %collective-permute-start = (f32[3,5,128,128]{3,2,1,0:T(8,128)}, f32[3,5,128,128]{3,2,1,0:T(8,128)S(1)}, u32[]{:S(2)}, u32[]{:S(2)}) collective-permute-start(f32[3,5,128,128]{3,2,1,0:T(8,128)} %get-tuple-element.34), channel_id=1, source_target_pairs={{0,8},{8,0},{16,24},{24,16},{1,9},{9,1},{17,25},{25,17},{2,10},{10... | collective-permute-start | bytes 2949128 | tf_op jit(solution)/shard_map/ppermute | solution.py:463
  14.6 23.5 %collective-permute-start.1 = (f32[3,5,128,128]{3,2,1,0:T(8,128)}, f32[3,5,128,128]{3,2,1,0:T(8,128)S(1)}, u32[]{:S(2)}, u32[]{:S(2)}) collective-permute-start(f32[3,5,128,128]{3,2,1,0:T(8,128)} %get-tuple-element.35), channel_id=1, source_target_pairs={{8,16},{16,8},{9,17},{17,9},{10,18},{18,10},{11,19},{19,11},{12,20... | collective-permute-start | bytes 2949128 | tf_op jit(solution)/shard_map/ppermute | solution.py:463
  29.4 25.9 %copy-start.1 = (f32[8,2]{0,1:T(2,128)S(1)}, f32[8,2]{0,1:T(2,128)}, u32[]{:S(2)}) copy-start(f32[8,2]{0,1:T(2,128)} %param.10) | copy-start | bytes 196
  29.4 19.5 %all-to-all-start.1 = ((f32[8,16,16,128]{3,2,1,0:T(8,128)}), f32[8,16,16,128]{3,2,1,0:T(8,128)S(1)}, u32[]{:S(2)}, u32[]{:S(2)}) async-start(f32[8,16,16,128]{3,2,1,0:T(8,128)} %temperature.1), calls=%async_computation.1 | async-start | bytes 2097152 | tf_op jit(solution)/shard_map/all_to_all | solution.py:556
  40.0 15.3 %collective-permute-start.2 = (f32[3,26,8,128]{3,2,1,0:T(8,128)}, f32[3,26,8,128]{3,2,1,0:T(8,128)S(1)}, u32[]{:S(2)}, u32[]{:S(2)}) collective-permute-start(f32[3,26,8,128]{3,2,1,0:T(8,128)} %get-tuple-element.36), channel_id=1, source_target_pairs={{0,1},{1,0},{2,3},{3,2},{4,5},{5,4},{6,7},{7,6},{8,9},{9,8},{10,11... | collective-permute-start | bytes 958472 | tf_op jit(solution)/shard_map/ppermute | solution.py:463
  41.7 28.8 %copy-start.2 = (f32[2]{0:T(128)S(1)}, f32[2]{0:T(128)}, u32[]{:S(2)}) copy-start(f32[2]{0:T(128)} %w_ref.3) | copy-start | bytes 28
  41.7 13.6 %collective-permute-start.3 = (f32[3,26,8,128]{3,2,1,0:T(8,128)}, f32[3,26,8,128]{3,2,1,0:T(8,128)}, u32[]{:S(2)}, u32[]{:S(2)}) collective-permute-start(f32[3,26,8,128]{3,2,1,0:T(8,128)} %get-tuple-element.37), channel_id=1, source_target_pairs={{1,2},{2,1},{3,4},{4,3},{5,6},{6,5},{7,0},{0,7},{9,10},{10,9},{11,... | collective-permute-start | bytes 958472 | tf_op jit(solution)/shard_map/ppermute | solution.py:463
  50.1 14.0 %collective-permute-start.4 = (f32[1,3,128,128]{3,2,1,0:T(8,128)S(1)}, f32[1,3,128,128]{3,2,1,0:T(8,128)S(1)}, u32[]{:S(2)}, u32[]{:S(2)}) collective-permute-start(f32[1,3,128,128]{3,2,1,0:T(8,128)S(1)} %get-tuple-element.40), channel_id=1, source_target_pairs={{0,8},{8,0},{16,24},{24,16},{1,9},{9,1},{17,25},{25,17},{2,10},{10... | collective-permute-start | bytes 589832 | tf_op jit(solution)/shard_map/ppermute | solution.py:463
  50.9 13.2 %collective-permute-start.5 = (f32[1,3,128,128]{3,2,1,0:T(8,128)S(1)}, f32[1,3,128,128]{3,2,1,0:T(8,128)S(1)}, u32[]{:S(2)}, u32[]{:S(2)}) collective-permute-start(f32[1,3,128,128]{3,2,1,0:T(8,128)S(1)} %get-tuple-element.41), channel_id=1, source_target_pairs={{8,16},{16,8},{9,17},{17,9},{10,18},{18,10},{11,19},{19,11},{12,20... | collective-permute-start | bytes 589832 | tf_op jit(solution)/shard_map/ppermute | solution.py:463
  64.2 16.0 %collective-permute-start.6 = (f32[1,22,8,128]{3,2,1,0:T(8,128)S(1)}, f32[1,22,8,128]{3,2,1,0:T(8,128)S(1)}, u32[]{:S(2)}, u32[]{:S(2)}) collective-permute-start(f32[1,22,8,128]{3,2,1,0:T(8,128)S(1)} %get-tuple-element.42), channel_id=1, source_target_pairs={{0,1},{1,0},{2,3},{3,2},{4,5},{5,4},{6,7},{7,6},{8,9},{9,8},{10,11... | collective-permute-start | bytes 270344 | tf_op jit(solution)/shard_map/ppermute | solution.py:463
  65.9 14.3 %collective-permute-start.7 = (f32[1,22,8,128]{3,2,1,0:T(8,128)S(1)}, f32[1,22,8,128]{3,2,1,0:T(8,128)S(1)}, u32[]{:S(2)}, u32[]{:S(2)}) collective-permute-start(f32[1,22,8,128]{3,2,1,0:T(8,128)S(1)} %get-tuple-element.43), channel_id=1, source_target_pairs={{1,2},{2,1},{3,4},{4,3},{5,6},{6,5},{7,0},{0,7},{9,10},{10,9},{11,... | collective-permute-start | bytes 270344 | tf_op jit(solution)/shard_map/ppermute | solution.py:463
  80.2 26.1 %copy-start = (f32[2,16,128,128]{3,2,1,0:T(8,128)S(1)}, f32[2,16,128,128]{3,2,1,0:T(8,128)}, u32[]{:S(2)}) copy-start(f32[2,16,128,128]{3,2,1,0:T(8,128)} %e_ref.7) | copy-start | bytes 6291460
